TPU v7x, 256 devices: a whole 4x4x8 slice. The times are simulated.
256 devices in a mesh: dp: 32 (over x_lo, z, core), feat: 8 (over y, x_hi).
Axes of the slice: x: 4 (x_hi: 2, x_lo: 2; x = x_hi * 2 + x_lo), y: 4, z: 8, core: 2. Of those that a mesh axis runs over, the one named last changes fastest.
Arguments:
- proj_grads: bfloat16 [8192, 16384], P('dp', 'feat'), may hold values from -1.25 to 1.25
- val_grads: bfloat16 [16384, 128], P('feat'), may hold values from -1.25 to 1.25
Outputs:
- interactions: bfloat16 [8192, 8192], P('dp', 'feat')
- data_scores: float32 [8192, 128], P('dp')
All inputs are finite; a program needn't handle non-finite values.
Results may differ from a plain program's by a relative error of at most 0.0006.
Values may be sent and summed in bfloat16 or wider, within the bound.
No kernel may reach another device: no remote copies, remote signals or barrier semaphores. Data moves between devices by JAX's collectives and lax.ppermute only.
A program may use at most 192 MiB of HBM per device.

v0:
```python
import functools

import jax
import jax.numpy as jnp
import numpy as np
from jax import lax
from jax.experimental import pallas as pl
from jax.experimental.pallas import tpu as pltpu
from jax.sharding import PartitionSpec as P


NZ, NF = 8, 8


def row_block(a, z, k):
    return (a % 2) * 2 * NZ + (z % NZ) * 2 + (k % 2)


PLACES = [(a, z, k) for a in range(2) for z in range(NZ) for k in range(2)]


def shift(to):
    return [(row_block(*p), row_block(*to(*p))) for p in PLACES]


FROM_ABOVE = shift(lambda a, z, k: (a, z - 1, k))
FROM_BELOW = shift(lambda a, z, k: (a, z + 1, k))
OTHER_COLUMN = shift(lambda a, z, k: (1 - a, z, k))
OTHER_CORE = shift(lambda a, z, k: (a, z, 1 - k))


CHIP_GROUPS = [[row_block(a, z, k) for a in range(2) for z in range(NZ)] for k in range(2)]


def pair_lists(a, z, k):
    o, j = 1 - a, 1 - k
    sel = k if a == 0 else j
    low = k if z < NZ // 2 else j
    blk = row_block
    one = [
        (blk(a, z - 1, k), blk(a, z + 1, k)),
        (blk(a, z - 1, j), blk(a, z + 1, k)),
        (blk(a, z - 1, k), blk(o, z, k)),
        (blk(a, z - 1, j), blk(o, z, k)),
        (blk(a, z, k), blk(a, z + 1, k)),
        (blk(a, z, j), blk(a, z + 1, k)),
        (blk(a, z, j), blk(a, z, k)),
        (blk(a, z, sel), blk(o, z, k)),
    ]
    two = [
        (blk(a, z - 2, k), blk(a, z + 1, k)),
        (blk(a, z - 2, j), blk(a, z + 1, k)),
        (blk(a, z - 2, k), blk(o, z, k)),
        (blk(a, z - 2, j), blk(o, z, k)),
        (blk(a, z - 2, low), blk(a, z + 2, k)),
        (blk(a, z - 1, k), blk(o, z + 2, k)),
        (blk(a, z - 1, j), blk(o, z + 2, k)),
        (blk(a, z - 2, sel), blk(o, z + 2, k)),
    ]
    return one, two


def colour_edges(edges, n_colours):
    at_src, at_dst = {}, {}
    colour = [None] * len(edges)

    def free(table, node):
        return next(c for c in range(n_colours) if (node, c) not in table)

    for e, (s, d) in enumerate(edges):
        c1, c2 = free(at_src, s), free(at_dst, d)
        if c1 != c2:
            path, node, side, c = [], d, 1, c1
            while True:
                nxt = (at_dst if side else at_src).get((node, c))
                if nxt is None:
                    break
                path.append(nxt)
                node = edges[nxt][0 if side else 1]
                side, c = 1 - side, c1 + c2 - c
            for q in path:
                at_src.pop((edges[q][0], colour[q]))
                at_dst.pop((edges[q][1], colour[q]))
            for q in path:
                colour[q] = c1 + c2 - colour[q]
                at_src[(edges[q][0], colour[q])] = q
                at_dst[(edges[q][1], colour[q])] = q
        colour[e] = c1
        at_src[(s, c1)] = e
        at_dst[(d, c1)] = e
    return colour


def hops(a, z, f, i, g):
    steps = ((f % 2 * 2 + a - g % 2 * 2 - i // (2 * NZ), 4), (f // 2 - g // 2, 4), (z - i // 2, NZ))
    return sum(min(d % n, -d % n) for d, n in steps)


def reducers():
    per = len(PLACES) // NF
    table = np.zeros((len(PLACES), 2, NF), np.int32)
    for a, z, k in PLACES:
        for round_, pairs in enumerate(pair_lists(a, z, k)):
            cost = [
                [
                    hops(a, z, f, r, c // per) ** 3 + hops(a, z, f, c, r // per) ** 3
                    for f in range(NF)
                ]
                for r, c in pairs
            ]
            at, better = list(range(NF)), True
            while better:
                better = False
                for p in range(NF):
                    for q in range(p):
                        now = cost[p][at[p]] + cost[q][at[q]]
                        if cost[p][at[q]] + cost[q][at[p]] < now:
                            at[p], at[q], better = at[q], at[p], True
            table[row_block(a, z, k), round_] = at
    return table


def routes(table):
    per = len(PLACES) // NF
    edges, what = [], []
    for p in PLACES:
        for round_, pairs in enumerate(pair_lists(*p)):
            for slot, (r, c) in enumerate(pairs):
                src = row_block(*p) * NF + int(table[row_block(*p), round_, slot])
                edges.append((src, r * NF + c // per))
                what.append((2 * round_, c % per))
                if not (round_ == 0 and slot == 6):
                    edges.append((src, c * NF + r // per))
                    what.append((2 * round_ + 1, r % per))
    colour = colour_edges(edges, 4)
    n = len(PLACES) * NF
    perms = [[] for _ in range(4)]
    sends = np.zeros((n, 4), np.int32)
    takes = np.full((n, 4), -1, np.int32)
    for (s, d), (item, at), c in zip(edges, what, colour):
        perms[c].append((s, d))
        sends[s, c] = item
        assert takes[d, at] < 0
        takes[d, at] = c
    for i in range(len(PLACES)):
        assert takes[i * NF + i // per, i % per] < 0
        takes[i * NF + i // per, i % per] = 4
    assert (takes >= 0).all()
    return perms, sends, takes


def exchange(value, axis, groups=None):
    return lax.all_to_all(
        value, axis, split_axis=0, concat_axis=0, tiled=True, axis_index_groups=groups
    )


def parts_of(x):
    high = x.astype(jnp.bfloat16)
    rest = x - high.astype(jnp.float32)
    mid = rest.astype(jnp.bfloat16)
    low = (rest - mid.astype(jnp.float32)).astype(jnp.bfloat16)
    return jnp.concatenate([high, mid, low], axis=-1)


def three(y):
    q = y.shape[-1] // 3
    return (y[:, 2 * q :] + y[:, q : 2 * q]) + y[:, :q]


def hdot_kernel(core, own, part, part_, first, mine, other):
    value = part[...] + part_[...]
    first[...] = value
    terms = parts_of(value)
    half = mine.shape[0]
    for at in range(2):
        rows = three(
            lax.dot_general(
                own[:, at * half : (at + 1) * half],
                terms,
                (((0,), (0,)), ((), ())),
                preferred_element_type=jnp.float32,
            )
        )

        @pl.when(core[0] == at)
        def _():
            mine[...] = rows

        @pl.when(core[0] != at)
        def _():
            other[...] = rows


def gdot_kernel(core, own, mine, other, first, one, one_, out):
    half = mine.shape[0]
    total = None
    for at in range(2):
        back = jnp.where(core[0] == at, mine[...], other[...])
        term = three(
            jnp.dot(
                own[:, at * half : (at + 1) * half], parts_of(back), preferred_element_type=jnp.float32
            )
        )
        total = term if total is None else total + term
    wide = own[...].astype(jnp.float32)
    rows, q = first.shape
    out[:rows] = total - jnp.sum(wide * wide, axis=1, keepdims=True) * first[...]
    square = one[2 * rows :] + one_[rows:]
    piece = square.shape[0]
    out[rows : rows + piece] = square[:, :q]
    out[rows + piece :] = square[:, q:]


def tile(left, right):
    return lax.dot_general(
        left, right, (((1,), (1,)), ((), ())), preferred_element_type=jnp.float32
    )


def products(plan, ins, flags):
    for left, right in plan:
        if isinstance(left, tuple):
            i, j, flag = left
            value = jnp.where(flags[flag] > 0, ins[i][...], ins[j][...])
        else:
            value = ins[left][...]
        if isinstance(right, tuple):
            against = jnp.concatenate([ins[i][...] for i in right], axis=0)
        else:
            against = ins[right][...]
        yield tile(value, against)


UP = (4, 5)
PLAN_1 = ((0, UP), (1, UP), (2, UP), (3, UP), (0, 6), (1, 6), ((2, 3, 0), 6), (3, 2))
SLOTS_1 = (0, 1, 4, 5, 2, 3, 7, 6)
PLAN_2A = ((0, (2, 3)), (1, (2, 3)), (0, 4), (1, 4))
PLAN_2B = (((0, 1, 1), (4, 5)), (2, (6, 7)), (3, (6, 7)), ((0, 1, 0), (6, 7)))


def kernel_1(flags, order, y, *refs):
    ins, outs, acc = refs[:7], refs[7:11], refs[11]
    for slot, product in zip(SLOTS_1, products(PLAN_1, ins, flags)):
        acc[order[0, slot]] = product
    square = tile(ins[2][...], ins[2][...])
    rows = square.shape[0]
    own = lax.broadcasted_iota(jnp.int32, (rows, rows), 0)
    other = lax.broadcasted_iota(jnp.int32, (rows, rows), 1)
    acc[NF] = jnp.where(own == other, 0.0, square)
    piece = 2 * rows // NF
    for dy, out in enumerate(outs):
        out[:rows] = acc[2 * dy]
        out[rows : 2 * rows] = acc[2 * dy + 1]
        at = pl.multiple_of((y[0] ^ dy) * piece, piece)
        out[2 * rows :] = acc[NF, pl.ds(at, piece)]


def kernel_2a(flags, *refs):
    for slot, product in enumerate(products(PLAN_2A, refs[:5], flags)):
        refs[5][slot] = product


def kernel_2b(flags, order, *refs):
    ins, early, along_y, along_x, acc = refs[:8], refs[8], refs[9:13], refs[13:15], refs[15]
    for slot, product in enumerate(products(PLAN_2B, ins, flags)):
        acc[order[1, NF // 2 + slot]] = product
    for slot in range(NF // 2):
        acc[order[1, slot]] = early[slot]
    cut = along_y[0].shape[1]
    for s in range(NF):
        along_y[s // 2][s % 2] = acc[s, :cut]
        along_x[s % 2][s // 2] = acc[s, cut:]


def mid_kernel(a, b, c, d, low, low_, keep, send, *lowers):
    upper = (a[...] + b[...]) + (c[...] + d[...])
    keep[...] = upper[0]
    send[...] = upper[1]
    for dy, out in enumerate(lowers):
        out[...] = low[dy] + low_[dy]


def items_kernel(sends, one_ref, one_ref_, up, up_, a, b, c, d, *outs):
    rows = one_ref.shape[1]
    one = one_ref[:rows] + one_ref_[:rows]
    lower = (a[...] + b[...]) + (c[...] + d[...])
    two = jnp.concatenate([up[...] + up_[...], lower], axis=0)
    choices = [x.astype(jnp.bfloat16) for x in (one, one.T, two, two.T)]
    for n, out in enumerate(outs):
        value = choices[3]
        for q in (2, 1, 0):
            value = jnp.where(sends[n] == q, choices[q], value)
        out[...] = value


def place_kernel(weight, takes, y, *refs):
    got, pieces, (total, total_, first), (out, scores), diagonal = (
        refs[:4], refs[4:8], refs[8:11], refs[11:13], refs[13]
    )
    rows = out.shape[0]
    piece = 2 * rows // NF
    half = first.shape[1]
    for dy, source in enumerate(pieces):
        at = pl.multiple_of((y[0] ^ dy) * piece, piece)
        diagonal[pl.ds(at, piece), :half] = source[rows : rows + piece].astype(jnp.bfloat16)
        diagonal[pl.ds(at, piece), half:] = source[rows + piece :].astype(jnp.bfloat16)
    values = [x[...] for x in got]
    for s in range(4):
        value = diagonal[...]
        for q in range(4):
            value = jnp.where(takes[s] == q, values[q], value)
        out[:, s * rows : (s + 1) * rows] = value
    scores[...] = first[...] - weight * (total[...] + total_[...])


def call(kernel, scalars, operands, outs, scratch=(), flops=0):
    vmem = pl.BlockSpec(memory_space=pltpu.VMEM)
    moved = sum(x.size * x.dtype.itemsize for x in (*operands, *outs))
    return pl.pallas_call(
        kernel,
        in_specs=[pl.BlockSpec(memory_space=pltpu.SMEM)] * len(scalars) + [vmem] * len(operands),
        out_specs=[vmem] * len(outs),
        out_shape=list(outs),
        scratch_shapes=list(scratch),
        compiler_params=pltpu.CompilerParams(vmem_limit_bytes=24 * 2**20),
        cost_estimate=pl.CostEstimate(flops=flops, bytes_accessed=moved, transcendentals=0),
    )(*scalars, *operands)


def array(dtype, *shape):
    return jax.ShapeDtypeStruct(shape, dtype)


def body(proj_grads, val_grads):
    rows, depth = proj_grads.shape
    pair_weight = 1.0 / rows**0.5
    tile_flops = 2 * rows * rows * depth
    table = reducers()
    perms, sends, takes = routes(table)
    dp = lax.axis_index("dp")
    feat = lax.axis_index("feat")
    me = dp * NF + feat
    column_0 = dp < 2 * NZ
    low_half = (dp // 2) % NZ < NZ // 2
    core = dp % 2
    flags = jnp.stack([column_0, low_half]).astype(jnp.int32)
    order = jnp.asarray(table)[dp] ^ feat
    y = feat // 2
    send = jnp.asarray(sends)[me]
    take = jnp.asarray(takes)[me]
    f32, bf16 = jnp.float32, jnp.bfloat16

    def move(x, perm):
        return lax.ppermute(x, "dp", perm)

    def from_feat(x, s):
        return lax.ppermute(x, "feat", [(f, f ^ s) for f in range(NF)])

    def over_y(parts, n=None):
        parts = [parts[0]] + [from_feat(parts[dy], 2 * dy) for dy in (1, 2, 3)]
        a, b, c, d = [p[:n] for p in parts]
        return (a + b) + (c + d), parts

    own = proj_grads
    cut = rows // 2
    up1 = [move(own[:cut], FROM_ABOVE), move(own[cut:], FROM_ABOVE)]
    down1 = move(own, FROM_BELOW)
    side = move(own, OTHER_COLUMN)
    own_ = move(own, OTHER_CORE)

    first = jnp.dot(own, val_grads, preferred_element_type=f32)
    first, _ = over_y([first] * 4)
    first_ = from_feat(first, 1)

    high = 3 * rows // 4
    up2 = [move(up1[0], FROM_ABOVE), move(up1[1], FROM_ABOVE)]
    down2 = move(down1, FROM_BELOW)
    down1_ = move(down1, OTHER_CORE)

    one = call(
        kernel_1,
        (flags, order, y[None]),
        (down1, down1_, own, own_, *up1, side),
        [array(f32, 2 * rows + 2 * rows // NF, rows)] * 4,
        [pltpu.VMEM((NF + 1, rows, rows), f32)],
        (NF + 1) * tile_flops,
    )
    one, _ = over_y(one)

    half = depth // 2
    q = first.shape[1]
    first, mine, other = call(
        hdot_kernel,
        (core[None],),
        (own, first, first_),
        [array(f32, rows, q), array(f32, half, q), array(f32, half, q)],
        flops=6 * rows * depth * q,
    )
    mine = mine + move(other, OTHER_CORE)
    chips = 2 * NZ
    mine = exchange(mine.reshape(chips, -1, mine.shape[1]), "dp", CHIP_GROUPS)
    mine = mine.sum(axis=0)
    mine = exchange(jnp.broadcast_to(mine, (chips, *mine.shape)), "dp", CHIP_GROUPS)
    mine = mine.reshape(half, -1)

    far = [move(up2[0], OTHER_COLUMN), move(up2[1], OTHER_COLUMN)]
    down2_ = move(down2, OTHER_CORE)
    (early,) = call(
        kernel_2a,
        (flags,),
        (down2, down2_, *up1, side),
        [array(f32, NF // 2, rows, rows)],
        flops=4 * tile_flops,
    )
    two = call(
        kernel_2b,
        (flags, order),
        (down2, down2_, down1, down1_, *up2, *far, early),
        [array(f32, 2, high, rows)] * 4 + [array(f32, 4, rows - high, rows)] * 2,
        [pltpu.VMEM((NF, rows, rows), f32)],
        4 * tile_flops,
    )
    upper = [two[0]] + [from_feat(two[dy], 2 * dy) for dy in (1, 2, 3)]
    lower_ = from_feat(two[5], 1)
    one_ = from_feat(one[rows:], 1)
    piece = 2 * rows // NF
    upper, send_, *lower = call(
        mid_kernel,
        (),
        (*upper, two[4], lower_),
        [array(f32, high, rows)] * 2 + [array(f32, rows - high, rows)] * 4,
    )
    upper_ = from_feat(send_, 1)
    lower = [lower[0]] + [from_feat(lower[dy], 2 * dy) for dy in (1, 2, 3)]

    other = move(mine, OTHER_CORE)
    (shared,) = call(
        gdot_kernel,
        (core[None],),
        (own, mine, other, first, one, one_),
        [array(f32, rows + 2 * piece, q)],
        flops=6 * rows * depth * q,
    )
    total, pieces = over_y([shared] * 4, rows)
    total_ = from_feat(total, 1)

    out = call(items_kernel, (send,), (one, one_, upper, upper_, *lower), [array(bf16, rows, rows)] * 4)
    got = []
    for c in range(4):
        got.append(lax.ppermute(out[c], ("dp", "feat"), perms[c]))
    return tuple(
        call(
            functools.partial(place_kernel, pair_weight),
            (take, y[None]),
            (*got, *pieces, total, total_, first),
            [array(bf16, rows, 4 * rows), array(f32, rows, q)],
            [pltpu.VMEM((rows, rows), bf16)],
        )
    )


def solution(mesh):
    return jax.shard_map(
        body,
        mesh=mesh,
        in_specs=(P("dp", "feat"), P("feat", None)),
        out_specs=(P("dp", "feat"), P("dp", None)),
        check_vma=False,
    )
```

profile of v0, /device:TPU:32, one launch (start us, length us, event | category | flops | bytes accessed | tf_op | source)
XLA Modules:
  0.0 208.6 jit_solution(1901645322638938670)
XLA Ops:
  0.7 2.0 collective-permute-start
  2.7 1.7 fusion.4
  4.3 3.3 %collective-permute-start.29 = (f32[256,128]{1,0:T(8,128)S(1)}, f32[256,128]{1,0:T(8,128)S(1)}, u32[]{:S(2)}, u32[]{:S(2)}) collective-permute-start(f32[256,128]{1,0:T(8,128)S(1)} %fusion.4), channel_id=1, source_target_pairs={{0,4},{1,5},{2,6},{3,7},{4,0},{5,1},{6,2},{7,3},{8,12},{9,13},{10,... | collective-permute-start | bytes 393224 | tf_op jit(solution)/shard_map/ppermute | solution.py:358
  7.6 1.1 collective-permute-start.30
  8.7 1.1 fusion.3
  9.9 1.6 collective-permute-done.29
  11.5 2.3 %collective-permute-done.30 = f32[256,128]{1,0:T(8,128)S(1)} collective-permute-done((f32[256,128]{1,0:T(8,128)S(1)}, f32[256,128]{1,0:T(8,128)S(1)}, u32[]{:S(2)}, u32[]{:S(2)}) %collective-permute-start.30) | collective-permute-done | bytes 131104 | tf_op jit(solution)/shard_map/ppermute | solution.py:358
  14.1 3.1 %collective-permute-start.31 = (f32[256,128]{1,0:T(8,128)S(1)}, f32[256,128]{1,0:T(8,128)S(1)}, u32[]{:S(2)}, u32[]{:S(2)}) collective-permute-start(f32[256,128]{1,0:T(8,128)S(1)} %add_add_fusion.1.part), channel_id=1, source_target_pairs={{0,1},{1,0},{2,3},{3,2},{4,5},{5,4},{6,7},{7,6},{8,9},{9,8},{10,11... | collective-permute-start | bytes 393224 | tf_op jit(solution)/shard_map/ppermute | solution.py:358
  17.2 3.4 %collective-permute-done.31.part_ = f32[256,128]{1,0:T(8,128)S(1)} collective-permute-done((f32[256,128]{1,0:T(8,128)S(1)}, f32[256,128]{1,0:T(8,128)S(1)}, u32[]{:S(2)}, u32[]{:S(2)}) %collective-permute-start.31) | collective-permute-done | bytes 131104 | tf_op jit(solution)/shard_map/ppermute | solution.py:358
  20.6 1.0 shard_map.73
  21.8 4.2 %collective-permute-done.refs_0_.refs_2_ = bf16[256,2048]{1,0:T(8,128)(2,1)} collective-permute-done((bf16[256,2048]{1,0:T(8,128)(2,1)}, bf16[256,2048]{1,0:T(8,128)(2,1)}, u32[]{:S(2)}, u32[]{:S(2)}) %collective-permute-start) | collective-permute-done | bytes 1048608 | tf_op jit(solution)/shard_map/ppermute | solution.py:355
  25.9 1.9 collective-permute-start.10
  27.9 1.5 collective-permute-start.5
  29.6 2.3 %collective-permute-start.4 = (bf16[128,2048]{1,0:T(8,128)(2,1)}, bf16[128,2048]{1,0:T(8,128)(2,1)}, u32[]{:S(2)}, u32[]{:S(2)}) collective-permute-start(bf16[128,2048]{1,0:T(8,128)(2,1)} %get-tuple-element.48), channel_id=1, source_target_pairs={{0,112},{8,120},{16,0},{24,8},{32,16},{40,24},{48,32},{56,40},{64,... | collective-permute-start | bytes 1572872 | tf_op jit(solution)/shard_map/ppermute | solution.py:355
  31.9 0.9 add.60
  32.8 8.8 %all-to-all-start = ((f32[16,64,128]{2,1,0:T(8,128)}), f32[16,64,128]{2,1,0:T(8,128)}, u32[]{:S(2)}, u32[]{:S(2)}) async-start(f32[16,64,128]{2,1,0:T(8,128)} %bitcast.14), calls=%async_computation | async-start | bytes 1048576 | tf_op jit(solution)/shard_map/all_to_all | solution.py:153
  41.6 4.8 %collective-permute-done.4.refs_5_.refs_3_ = bf16[128,2048]{1,0:T(8,128)(2,1)} collective-permute-done((bf16[128,2048]{1,0:T(8,128)(2,1)}, bf16[128,2048]{1,0:T(8,128)(2,1)}, u32[]{:S(2)}, u32[]{:S(2)}) %collective-permute-start.4) | collective-permute-done | bytes 524320 | tf_op jit(solution)/shard_map/ppermute | solution.py:355
  46.4 6.8 %collective-permute-start.12 = (bf16[128,2048]{1,0:T(8,128)(2,1)S(1)}, bf16[128,2048]{1,0:T(8,128)(2,1)}, u32[]{:S(2)}, u32[]{:S(2)}) collective-permute-start(bf16[128,2048]{1,0:T(8,128)(2,1)S(1)} %collective-permute-done.3.refs_4_.refs_2_), channel_id=1, source_target_pairs={{0,112},{8,120},{16,0},{24,8},{32,16},{40,24},{48,32},{56,40},{64,... | collective-permute-start | bytes 1572872 | tf_op jit(solution)/shard_map/ppermute | solution.py:355
  53.9 1.1 collective-permute-done.10.refs_0_
  55.0 1.1 collective-permute-done.5.refs_6_.refs_4_
  56.2 6.0 %shard_map.68 = (f32[576,256]{1,0:T(8,128)S(1)}, f32[576,256]{1,0:T(8,128)S(1)}, f32[576,256]{1,0:T(8,128)}, f32[576,256]{1,0:T(8,128)S(1)}) custom-call(s32[2]{0:T(128)S(1)} %add_convert_fusion.flags, s32[2,8]{1,0:T(2,128)S(1)} %xor_bitcast_fusion.order, s32[1]{0:T(128)} %bitcast.1.y, bf16[256,2048]{1,0:T(8,128)(2,1)} %collective-permute-done.refs_0_.refs_2_, ...), custom_call_target="tpu_custom_call" | custom-call | flops 2415919104 | bytes 8650752 | tf_op jit(solution)/shard_map/pallas_call | solution.py:320
  62.1 0.8 copy-done.2
  63.0 0.8 copy-done.16
  63.8 0.9 copy-done.17
  64.7 3.2 %collective-permute-start.7 = (f32[576,256]{1,0:T(8,128)}, f32[576,256]{1,0:T(8,128)}, u32[]{:S(2)}, u32[]{:S(2)}) collective-permute-start(f32[576,256]{1,0:T(8,128)} %get-tuple-element.27), channel_id=1, source_target_pairs={{0,4},{1,5},{2,6},{3,7},{4,0},{5,1},{6,2},{7,3},{8,12},{9,13},{10,... | collective-permute-start | bytes 1769480 | tf_op jit(solution)/shard_map/ppermute | solution.py:358
  67.9 1.1 reduce_sum.9
  68.9 0.8 broadcast_in_dim.13
  69.8 14.3 %all-to-all-start.1 = ((f32[16,64,128]{2,1,0:T(8,128)}), f32[16,64,128]{2,1,0:T(8,128)}, u32[]{:S(2)}, u32[]{:S(2)}) async-start(f32[16,64,128]{2,1,0:T(8,128)} %broadcast_in_dim.13), calls=%async_computation.1 | async-start | bytes 1048576 | tf_op jit(solution)/shard_map/all_to_all | solution.py:153
  84.3 1.1 collective-permute-start.8
  85.4 23.5 %collective-permute-done.13.refs_5_ = bf16[128,2048]{1,0:T(8,128)(2,1)} collective-permute-done((bf16[128,2048]{1,0:T(8,128)(2,1)}, bf16[128,2048]{1,0:T(8,128)(2,1)}, u32[]{:S(2)}, u32[]{:S(2)}) %collective-permute-start.13) | collective-permute-done | bytes 524320 | tf_op jit(solution)/shard_map/ppermute | solution.py:355
  108.9 1.5 collective-permute-start.14
  110.9 1.4 add_add_fusion.one_ref.one
  112.3 0.8 slice.28
  113.1 2.7 %collective-permute-start.9 = (f32[320,256]{1,0:T(8,128)}, f32[320,256]{1,0:T(8,128)S(1)}, u32[]{:S(2)}, u32[]{:S(2)}) collective-permute-start(f32[320,256]{1,0:T(8,128)} %slice.28), channel_id=1, source_target_pairs={{0,1},{1,0},{2,3},{3,2},{4,5},{5,4},{6,7},{7,6},{8,9},{9,8},{10,11... | collective-permute-start | bytes 983048 | tf_op jit(solution)/shard_map/ppermute | solution.py:358
  115.8 1.0 copy-done.7
  116.9 3.0 %shard_map.69.refs_8_ = f32[4,256,256]{2,1,0:T(8,128)S(1)} custom-call(s32[2]{0:T(128)S(1)} %add_convert_fusion.flags, bf16[256,2048]{1,0:T(8,128)(2,1)S(1)} %collective-permute-done.10.refs_0_, bf16[256,2048]{1,0:T(8,128)(2,1)} %collective-permute-done.11.refs_1_, bf16[128,2048]{1,0:T(8,128)(2,1)S(1)} %copy-done.7, ...), custom_call_target="tpu_custom_call" | custom-call | flops 1073741824 | bytes 5242880 | tf_op jit(solution)/shard_map/pallas_call | solution.py:320
  119.9 4.1 %collective-permute-done.14.refs_6_ = bf16[128,2048]{1,0:T(8,128)(2,1)} collective-permute-done((bf16[128,2048]{1,0:T(8,128)(2,1)}, bf16[128,2048]{1,0:T(8,128)(2,1)}, u32[]{:S(2)}, u32[]{:S(2)}) %collective-permute-start.14) | collective-permute-done | bytes 524320 | tf_op jit(solution)/shard_map/ppermute | solution.py:355
  124.0 11.2 %collective-permute-done.15.refs_7_ = bf16[128,2048]{1,0:T(8,128)(2,1)} collective-permute-done((bf16[128,2048]{1,0:T(8,128)(2,1)}, bf16[128,2048]{1,0:T(8,128)(2,1)}, u32[]{:S(2)}, u32[]{:S(2)}) %collective-permute-start.15) | collective-permute-done | bytes 524320 | tf_op jit(solution)/shard_map/ppermute | solution.py:355
  135.2 4.9 %shard_map.70 = (f32[2,192,256]{2,1,0:T(8,128)S(1)}, f32[2,192,256]{2,1,0:T(8,128)S(1)}, f32[2,192,256]{2,1,0:T(8,128)}, f32[2,192,256]{2,1,0:T(8,128)}, f32[4,6...) custom-call(s32[2]{0:T(128)S(1)} %add_convert_fusion.flags, s32[2,8]{1,0:T(2,128)S(1)} %xor_bitcast_fusion.order, ...), custom_call_target="tpu_custom_call" | custom-call | flops 1073741824 | bytes 9437184 | tf_op jit(solution)/shard_map/pallas_call | solution.py:320
  140.1 0.8 collective-permute-start.16
  140.9 2.7 %collective-permute-start.19 = (f32[4,64,256]{2,1,0:T(8,128)S(1)}, f32[4,64,256]{2,1,0:T(8,128)S(1)}, u32[]{:S(2)}, u32[]{:S(2)}) collective-permute-start(f32[4,64,256]{2,1,0:T(8,128)S(1)} %get-tuple-element.34), channel_id=1, source_target_pairs={{0,1},{1,0},{2,3},{3,2},{4,5},{5,4},{6,7},{7,6},{8,9},{9,8},{10,11... | collective-permute-start | bytes 786440 | tf_op jit(solution)/shard_map/ppermute | solution.py:358
  143.6 1.8 collective-permute-start.17
  145.5 2.2 %collective-permute-start.18 = (f32[2,192,256]{2,1,0:T(8,128)}, f32[2,192,256]{2,1,0:T(8,128)}, u32[]{:S(2)}, u32[]{:S(2)}) collective-permute-start(f32[2,192,256]{2,1,0:T(8,128)} %get-tuple-element.32), channel_id=1, source_target_pairs={{0,6},{1,7},{2,4},{3,5},{4,2},{5,3},{6,0},{7,1},{8,14},{9,15},{10,... | collective-permute-start | bytes 1179656 | tf_op jit(solution)/shard_map/ppermute | solution.py:358
  147.6 1.8 shard_map.74.refs_4_
  150.3 2.5 %collective-permute-start.35 = (f32[384,128]{1,0:T(8,128)S(1)}, f32[384,128]{1,0:T(8,128)}, u32[]{:S(2)}, u32[]{:S(2)}) collective-permute-start(f32[384,128]{1,0:T(8,128)S(1)} %shard_map.74.refs_4_), channel_id=1, source_target_pairs={{0,4},{1,5},{2,6},{3,7},{4,0},{5,1},{6,2},{7,3},{8,12},{9,13},{10,... | collective-permute-start | bytes 589832 | tf_op jit(solution)/shard_map/ppermute | solution.py:358
  153.6 2.2 %collective-permute-start.36 = (f32[384,128]{1,0:T(8,128)S(1)}, f32[384,128]{1,0:T(8,128)}, u32[]{:S(2)}, u32[]{:S(2)}) collective-permute-start(f32[384,128]{1,0:T(8,128)S(1)} %shard_map.74.refs_4_), channel_id=1, source_target_pairs={{0,6},{1,7},{2,4},{3,5},{4,2},{5,3},{6,0},{7,1},{8,14},{9,15},{10,... | collective-permute-start | bytes 589832 | tf_op jit(solution)/shard_map/ppermute | solution.py:358
  156.4 4.5 %collective-permute-done.17.c = f32[2,192,256]{2,1,0:T(8,128)} collective-permute-done((f32[2,192,256]{2,1,0:T(8,128)}, f32[2,192,256]{2,1,0:T(8,128)}, u32[]{:S(2)}, u32[]{:S(2)}) %collective-permute-start.17) | collective-permute-done | bytes 393248 | tf_op jit(solution)/shard_map/ppermute | solution.py:358
  161.0 7.3 %collective-permute-done.18.d = f32[2,192,256]{2,1,0:T(8,128)} collective-permute-done((f32[2,192,256]{2,1,0:T(8,128)}, f32[2,192,256]{2,1,0:T(8,128)}, u32[]{:S(2)}, u32[]{:S(2)}) %collective-permute-start.18) | collective-permute-done | bytes 393248 | tf_op jit(solution)/shard_map/ppermute | solution.py:358
  168.3 1.0 copy-done.9
  169.3 1.0 copy-done.11
  170.3 0.9 copy-done.13
  171.2 0.9 copy-done.15
  172.2 1.2 shard_map.71
  173.4 0.9 collective-permute-start.20
  174.3 4.3 %collective-permute-start.22 = (f32[64,256]{1,0:T(8,128)S(1)}, f32[64,256]{1,0:T(8,128)S(1)}, u32[]{:S(2)}, u32[]{:S(2)}) collective-permute-start(f32[64,256]{1,0:T(8,128)S(1)} %get-tuple-element.39), channel_id=1, source_target_pairs={{0,4},{1,5},{2,6},{3,7},{4,0},{5,1},{6,2},{7,3},{8,12},{9,13},{10,... | collective-permute-start | bytes 196616 | tf_op jit(solution)/shard_map/ppermute | solution.py:358
  179.0 1.1 fusion.refs_8_
  180.1 2.8 %collective-permute-start.37 = (f32[256,128]{1,0:T(8,128)S(1)}, f32[256,128]{1,0:T(8,128)S(1)}, u32[]{:S(2)}, u32[]{:S(2)}) collective-permute-start(f32[256,128]{1,0:T(8,128)S(1)} %fusion.refs_8_), channel_id=1, source_target_pairs={{0,1},{1,0},{2,3},{3,2},{4,5},{5,4},{6,7},{7,6},{8,9},{9,8},{10,11... | collective-permute-start | bytes 393224 | tf_op jit(solution)/shard_map/ppermute | solution.py:358
  182.9 1.3 collective-permute-done.23.d
  184.9 4.5 %collective-permute-start.24 = (bf16[256,256]{1,0:T(8,128)(2,1)S(1)}, bf16[256,256]{1,0:T(8,128)(2,1)S(1)}, u32[]{:S(2)}, u32[]{:S(2)}) collective-permute-start(bf16[256,256]{1,0:T(8,128)(2,1)S(1)} %get-tuple-element.41), channel_id=1, source_target_pairs={{1,112},{4,116},{0,16},{5,4},{2,19},{6,131},{3,117},{7,125},{9,120... | collective-permute-start | bytes 393224 | tf_op jit(solution)/shard_map/ppermute | solution.py:451
  189.4 6.1 %collective-permute-start.25 = (bf16[256,256]{1,0:T(8,128)(2,1)S(1)}, bf16[256,256]{1,0:T(8,128)(2,1)S(1)}, u32[]{:S(2)}, u32[]{:S(2)}) collective-permute-start(bf16[256,256]{1,0:T(8,128)(2,1)S(1)} %get-tuple-element.42), channel_id=1, source_target_pairs={{1,19},{4,131},{2,124},{0,0},{6,8},{5,128},{3,163},{10,104},{8,27}... | collective-permute-start | bytes 393224 | tf_op jit(solution)/shard_map/ppermute | solution.py:451
  195.5 1.9 collective-permute-start.26
  197.4 1.9 collective-permute-start.27
  200.1 6.3 %collective-permute-done.27.refs_3_ = bf16[256,256]{1,0:T(8,128)(2,1)S(1)} collective-permute-done((bf16[256,256]{1,0:T(8,128)(2,1)S(1)}, bf16[256,256]{1,0:T(8,128)(2,1)S(1)}, u32[]{:S(2)}, u32[]{:S(2)}) %collective-permute-start.27) | collective-permute-done | bytes 131104 | tf_op jit(solution)/shard_map/ppermute | solution.py:451
  206.4 2.1 %shard_map.75 = (bf16[256,1024]{1,0:T(8,128)(2,1)}, f32[256,128]{1,0:T(8,128)}) custom-call(s32[4]{0:T(128)S(1)} %fusion.1.takes, s32[1]{0:T(128)} %bitcast.1.y, bf16[256,256]{1,0:T(8,128)(2,1)S(1)} %collective-permute-done.24.refs_0_, bf16[256,256]{1,0:T(8,128)(2,1)S(1)} %collective-permute-done.25.refs_1_, ...), custom_call_target="tpu_custom_call" | custom-call | bytes 2359296 | tf_op jit(solution)/shard_map/pallas_call | solution.py:320
  (73 shorter events, 6.4 us)
Async XLA Ops:
  0.6 2.0 copy-start
  0.6 8.0 %copy-start.1 = (bf16[256,2048]{1,0:T(8,128)(2,1)S(1)}, bf16[256,2048]{1,0:T(8,128)(2,1)}, u32[]{:S(2)}) copy-start(bf16[256,2048]{1,0:T(8,128)(2,1)} %own.3) | copy-start | bytes 3145732
  0.7 25.3 %collective-permute-start = (bf16[256,2048]{1,0:T(8,128)(2,1)}, bf16[256,2048]{1,0:T(8,128)(2,1)}, u32[]{:S(2)}, u32[]{:S(2)}) collective-permute-start(bf16[256,2048]{1,0:T(8,128)(2,1)} %own.3), channel_id=1, source_target_pairs={{0,16},{8,24},{16,32},{24,40},{32,48},{40,56},{48,64},{56,72},{64,... | collective-permute-start | bytes 3145736 | tf_op jit(solution)/shard_map/ppermute | solution.py:355
  4.3 7.2 %collective-permute-start.29 = (f32[256,128]{1,0:T(8,128)S(1)}, f32[256,128]{1,0:T(8,128)S(1)}, u32[]{:S(2)}, u32[]{:S(2)}) collective-permute-start(f32[256,128]{1,0:T(8,128)S(1)} %fusion.4), channel_id=1, source_target_pairs={{0,4},{1,5},{2,6},{3,7},{4,0},{5,1},{6,2},{7,3},{8,12},{9,13},{10,... | collective-permute-start | bytes 393224 | tf_op jit(solution)/shard_map/ppermute | solution.py:358
  7.6 6.2 %collective-permute-start.30 = (f32[256,128]{1,0:T(8,128)S(1)}, f32[256,128]{1,0:T(8,128)S(1)}, u32[]{:S(2)}, u32[]{:S(2)}) collective-permute-start(f32[256,128]{1,0:T(8,128)S(1)} %fusion.4), channel_id=1, source_target_pairs={{0,6},{1,7},{2,4},{3,5},{4,2},{5,3},{6,0},{7,1},{8,14},{9,15},{10,... | collective-permute-start | bytes 393224 | tf_op jit(solution)/shard_map/ppermute | solution.py:358
  8.7 5.4 %collective-permute-start.28 = (f32[256,128]{1,0:T(8,128)S(1)}, f32[256,128]{1,0:T(8,128)S(1)}, u32[]{:S(2)}, u32[]{:S(2)}) collective-permute-start(f32[256,128]{1,0:T(8,128)S(1)} %fusion.4), channel_id=1, source_target_pairs={{0,2},{1,3},{2,0},{3,1},{4,6},{5,7},{6,4},{7,5},{8,10},{9,11},{10,... | collective-permute-start | bytes 393224 | tf_op jit(solution)/shard_map/ppermute | solution.py:358
  9.8 19.6 %collective-permute-start.3 = (bf16[128,2048]{1,0:T(8,128)(2,1)}, bf16[128,2048]{1,0:T(8,128)(2,1)S(1)}, u32[]{:S(2)}, u32[]{:S(2)}) collective-permute-start(bf16[128,2048]{1,0:T(8,128)(2,1)} %get-tuple-element.49), channel_id=1, source_target_pairs={{0,112},{8,120},{16,0},{24,8},{32,16},{40,24},{48,32},{56,40},{64,... | collective-permute-start | bytes 1572872 | tf_op jit(solution)/shard_map/ppermute | solution.py:355
  14.1 6.6 %collective-permute-start.31 = (f32[256,128]{1,0:T(8,128)S(1)}, f32[256,128]{1,0:T(8,128)S(1)}, u32[]{:S(2)}, u32[]{:S(2)}) collective-permute-start(f32[256,128]{1,0:T(8,128)S(1)} %add_add_fusion.1.part), channel_id=1, source_target_pairs={{0,1},{1,0},{2,3},{3,2},{4,5},{5,4},{6,7},{7,6},{8,9},{9,8},{10,11... | collective-permute-start | bytes 393224 | tf_op jit(solution)/shard_map/ppermute | solution.py:358
  21.6 11.1 %copy-start.3 = (f32[256,128]{1,0:T(8,128)}, f32[256,128]{1,0:T(8,128)S(1)}, u32[]{:S(2)}) copy-start(f32[256,128]{1,0:T(8,128)S(1)} %get-tuple-element.47.first.refs_10_) | copy-start | bytes 393220
  21.7 7.9 %collective-permute-start.32 = (f32[1024,128]{1,0:T(8,128)S(1)}, f32[1024,128]{1,0:T(8,128)S(1)}, u32[]{:S(2)}, u32[]{:S(2)}) collective-permute-start(f32[1024,128]{1,0:T(8,128)S(1)} %get-tuple-element.46), channel_id=1, source_target_pairs={{0,8},{8,0},{16,24},{24,16},{32,40},{40,32},{48,56},{56,48},{64,72... | collective-permute-start | bytes 1572872 | tf_op jit(solution)/shard_map/ppermute | solution.py:355
  25.9 29.1 %collective-permute-start.10 = (bf16[256,2048]{1,0:T(8,128)(2,1)}, bf16[256,2048]{1,0:T(8,128)(2,1)S(1)}, u32[]{:S(2)}, u32[]{:S(2)}) collective-permute-start(bf16[256,2048]{1,0:T(8,128)(2,1)} %collective-permute-done.refs_0_.refs_2_), channel_id=1, source_target_pairs={{0,16},{8,24},{16,32},{24,40},{32,48},{40,56},{48,64},{56,72},{64,... | collective-permute-start | bytes 3145736 | tf_op jit(solution)/shard_map/ppermute | solution.py:355
  27.9 27.2 %collective-permute-start.2 = (bf16[256,2048]{1,0:T(8,128)(2,1)S(1)}, bf16[256,2048]{1,0:T(8,128)(2,1)}, u32[]{:S(2)}, u32[]{:S(2)}) collective-permute-start(bf16[256,2048]{1,0:T(8,128)(2,1)S(1)} %copy-done.1), channel_id=1, source_target_pairs={{0,8},{8,0},{16,24},{24,16},{32,40},{40,32},{48,56},{56,48},{64,72... | collective-permute-start | bytes 3145736 | tf_op jit(solution)/shard_map/ppermute | solution.py:355
  27.9 28.3 %collective-permute-start.5 = (bf16[256,2048]{1,0:T(8,128)(2,1)S(1)}, bf16[256,2048]{1,0:T(8,128)(2,1)}, u32[]{:S(2)}, u32[]{:S(2)}) collective-permute-start(bf16[256,2048]{1,0:T(8,128)(2,1)S(1)} %copy-done.1), channel_id=1, source_target_pairs={{0,128},{8,136},{16,144},{24,152},{32,160},{40,168},{48,176},{56,1... | collective-permute-start | bytes 3145736 | tf_op jit(solution)/shard_map/ppermute | solution.py:355
  29.4 26.8 %copy-start.6 = (bf16[128,2048]{1,0:T(8,128)(2,1)}, bf16[128,2048]{1,0:T(8,128)(2,1)S(1)}, u32[]{:S(2)}) copy-start(bf16[128,2048]{1,0:T(8,128)(2,1)S(1)} %collective-permute-done.3.refs_4_.refs_2_) | copy-start | bytes 1572868
  29.4 26.8 %collective-permute-start.1 = (bf16[256,2048]{1,0:T(8,128)(2,1)}, bf16[256,2048]{1,0:T(8,128)(2,1)}, u32[]{:S(2)}, u32[]{:S(2)}) collective-permute-start(bf16[256,2048]{1,0:T(8,128)(2,1)} %collective-permute-done.refs_0_.refs_2_), channel_id=1, source_target_pairs={{0,8},{8,0},{16,24},{24,16},{32,40},{40,32},{48,56},{56,48},{64,72... | collective-permute-start | bytes 3145736 | tf_op jit(solution)/shard_map/ppermute | solution.py:355
  29.6 16.8 %collective-permute-start.4 = (bf16[128,2048]{1,0:T(8,128)(2,1)}, bf16[128,2048]{1,0:T(8,128)(2,1)}, u32[]{:S(2)}, u32[]{:S(2)}) collective-permute-start(bf16[128,2048]{1,0:T(8,128)(2,1)} %get-tuple-element.48), channel_id=1, source_target_pairs={{0,112},{8,120},{16,0},{24,8},{32,16},{40,24},{48,32},{56,40},{64,... | collective-permute-start | bytes 1572872 | tf_op jit(solution)/shard_map/ppermute | solution.py:355
  32.8 35.1 %all-to-all-start = ((f32[16,64,128]{2,1,0:T(8,128)}), f32[16,64,128]{2,1,0:T(8,128)}, u32[]{:S(2)}, u32[]{:S(2)}) async-start(f32[16,64,128]{2,1,0:T(8,128)} %bitcast.14), calls=%async_computation | async-start | bytes 1048576 | tf_op jit(solution)/shard_map/all_to_all | solution.py:153
  46.4 39.0 %collective-permute-start.12 = (bf16[128,2048]{1,0:T(8,128)(2,1)S(1)}, bf16[128,2048]{1,0:T(8,128)(2,1)}, u32[]{:S(2)}, u32[]{:S(2)}) collective-permute-start(bf16[128,2048]{1,0:T(8,128)(2,1)S(1)} %collective-permute-done.3.refs_4_.refs_2_), channel_id=1, source_target_pairs={{0,112},{8,120},{16,0},{24,8},{32,16},{40,24},{48,32},{56,40},{64,... | collective-permute-start | bytes 1572872 | tf_op jit(solution)/shard_map/ppermute | solution.py:355
  55.0 60.8 %collective-permute-start.11 = (bf16[256,2048]{1,0:T(8,128)(2,1)S(1)}, bf16[256,2048]{1,0:T(8,128)(2,1)}, u32[]{:S(2)}, u32[]{:S(2)}) collective-permute-start(bf16[256,2048]{1,0:T(8,128)(2,1)S(1)} %collective-permute-done.10.refs_0_), channel_id=1, source_target_pairs={{0,8},{8,0},{16,24},{24,16},{32,40},{40,32},{48,56},{56,48},{64,72... | collective-permute-start | bytes 3145736 | tf_op jit(solution)/shard_map/ppermute | solution.py:355
  62.1 0.8 copy-start.2
  63.0 0.8 copy-start.16
  63.8 0.9 copy-start.17
  64.7 45.7 %collective-permute-start.7 = (f32[576,256]{1,0:T(8,128)}, f32[576,256]{1,0:T(8,128)}, u32[]{:S(2)}, u32[]{:S(2)}) collective-permute-start(f32[576,256]{1,0:T(8,128)} %get-tuple-element.27), channel_id=1, source_target_pairs={{0,4},{1,5},{2,6},{3,7},{4,0},{5,1},{6,2},{7,3},{8,12},{9,13},{10,... | collective-permute-start | bytes 1769480 | tf_op jit(solution)/shard_map/ppermute | solution.py:358
  69.8 46.0 %all-to-all-start.1 = ((f32[16,64,128]{2,1,0:T(8,128)}), f32[16,64,128]{2,1,0:T(8,128)}, u32[]{:S(2)}, u32[]{:S(2)}) async-start(f32[16,64,128]{2,1,0:T(8,128)} %broadcast_in_dim.13), calls=%async_computation.1 | async-start | bytes 1048576 | tf_op jit(solution)/shard_map/all_to_all | solution.py:153
  84.1 24.8 %collective-permute-start.13 = (bf16[128,2048]{1,0:T(8,128)(2,1)}, bf16[128,2048]{1,0:T(8,128)(2,1)}, u32[]{:S(2)}, u32[]{:S(2)}) collective-permute-start(bf16[128,2048]{1,0:T(8,128)(2,1)} %collective-permute-done.4.refs_5_.refs_3_), channel_id=1, source_target_pairs={{0,112},{8,120},{16,0},{24,8},{32,16},{40,24},{48,32},{56,40},{64,... | collective-permute-start | bytes 1572872 | tf_op jit(solution)/shard_map/ppermute | solution.py:355
  84.3 26.6 %collective-permute-start.8 = (f32[576,256]{1,0:T(8,128)}, f32[576,256]{1,0:T(8,128)S(1)}, u32[]{:S(2)}, u32[]{:S(2)}) collective-permute-start(f32[576,256]{1,0:T(8,128)} %copy-done.17), channel_id=1, source_target_pairs={{0,6},{1,7},{2,4},{3,5},{4,2},{5,3},{6,0},{7,1},{8,14},{9,15},{10,... | collective-permute-start | bytes 1769480 | tf_op jit(solution)/shard_map/ppermute | solution.py:358
  85.4 25.5 %collective-permute-start.6 = (f32[576,256]{1,0:T(8,128)}, f32[576,256]{1,0:T(8,128)S(1)}, u32[]{:S(2)}, u32[]{:S(2)}) collective-permute-start(f32[576,256]{1,0:T(8,128)} %copy-done.16), channel_id=1, source_target_pairs={{0,2},{1,3},{2,0},{3,1},{4,6},{5,7},{6,4},{7,5},{8,10},{9,11},{10,... | collective-permute-start | bytes 1769480 | tf_op jit(solution)/shard_map/ppermute | solution.py:358
  108.9 15.1 %collective-permute-start.14 = (bf16[128,2048]{1,0:T(8,128)(2,1)}, bf16[128,2048]{1,0:T(8,128)(2,1)}, u32[]{:S(2)}, u32[]{:S(2)}) collective-permute-start(bf16[128,2048]{1,0:T(8,128)(2,1)} %collective-permute-done.12.refs_4_), channel_id=1, source_target_pairs={{0,128},{8,136},{16,144},{24,152},{32,160},{40,168},{48,176},{56,1... | collective-permute-start | bytes 1572872 | tf_op jit(solution)/shard_map/ppermute | solution.py:355
  110.4 24.9 %collective-permute-start.15 = (bf16[128,2048]{1,0:T(8,128)(2,1)}, bf16[128,2048]{1,0:T(8,128)(2,1)}, u32[]{:S(2)}, u32[]{:S(2)}) collective-permute-start(bf16[128,2048]{1,0:T(8,128)(2,1)} %collective-permute-done.13.refs_5_), channel_id=1, source_target_pairs={{0,128},{8,136},{16,144},{24,152},{32,160},{40,168},{48,176},{56,1... | collective-permute-start | bytes 1572872 | tf_op jit(solution)/shard_map/ppermute | solution.py:355
  113.1 32.4 %collective-permute-start.9 = (f32[320,256]{1,0:T(8,128)}, f32[320,256]{1,0:T(8,128)S(1)}, u32[]{:S(2)}, u32[]{:S(2)}) collective-permute-start(f32[320,256]{1,0:T(8,128)} %slice.28), channel_id=1, source_target_pairs={{0,1},{1,0},{2,3},{3,2},{4,5},{5,4},{6,7},{7,6},{8,9},{9,8},{10,11... | collective-permute-start | bytes 983048 | tf_op jit(solution)/shard_map/ppermute | solution.py:358
  115.8 31.8 %collective-permute-start.33 = (f32[1024,128]{1,0:T(8,128)}, f32[1024,128]{1,0:T(8,128)S(1)}, u32[]{:S(2)}, u32[]{:S(2)}) collective-permute-start(f32[1024,128]{1,0:T(8,128)} %bitcast.8.mine), channel_id=1, source_target_pairs={{0,8},{8,0},{16,24},{24,16},{32,40},{40,32},{48,56},{56,48},{64,72... | collective-permute-start | bytes 1572872 | tf_op jit(solution)/shard_map/ppermute | solution.py:355
  115.8 1.0 copy-start.7
  119.9 27.8 %copy-start.4 = (f32[256,128]{1,0:T(8,128)S(1)}, f32[256,128]{1,0:T(8,128)}, u32[]{:S(2)}) copy-start(f32[256,128]{1,0:T(8,128)} %copy-done.3) | copy-start | bytes 393220
  140.1 9.4 %copy-start.8 = (f32[2,192,256]{2,1,0:T(8,128)}, f32[2,192,256]{2,1,0:T(8,128)S(1)}, u32[]{:S(2)}) copy-start(f32[2,192,256]{2,1,0:T(8,128)S(1)} %get-tuple-element.29.a) | copy-start | bytes 1179652
  140.1 9.4 %copy-start.12 = (f32[4,64,256]{2,1,0:T(8,128)}, f32[4,64,256]{2,1,0:T(8,128)S(1)}, u32[]{:S(2)}) copy-start(f32[4,64,256]{2,1,0:T(8,128)S(1)} %get-tuple-element.33.low) | copy-start | bytes 786436
  140.1 12.7 %collective-permute-start.16 = (f32[2,192,256]{2,1,0:T(8,128)S(1)}, f32[2,192,256]{2,1,0:T(8,128)S(1)}, u32[]{:S(2)}, u32[]{:S(2)}) collective-permute-start(f32[2,192,256]{2,1,0:T(8,128)S(1)} %get-tuple-element.30), channel_id=1, source_target_pairs={{0,2},{1,3},{2,0},{3,1},{4,6},{5,7},{6,4},{7,5},{8,10},{9,11},{10,... | collective-permute-start | bytes 1179656 | tf_op jit(solution)/shard_map/ppermute | solution.py:358
  140.9 8.7 %collective-permute-start.19 = (f32[4,64,256]{2,1,0:T(8,128)S(1)}, f32[4,64,256]{2,1,0:T(8,128)S(1)}, u32[]{:S(2)}, u32[]{:S(2)}) collective-permute-start(f32[4,64,256]{2,1,0:T(8,128)S(1)} %get-tuple-element.34), channel_id=1, source_target_pairs={{0,1},{1,0},{2,3},{3,2},{4,5},{5,4},{6,7},{7,6},{8,9},{9,8},{10,11... | collective-permute-start | bytes 786440 | tf_op jit(solution)/shard_map/ppermute | solution.py:358
  143.6 17.4 %collective-permute-start.17 = (f32[2,192,256]{2,1,0:T(8,128)}, f32[2,192,256]{2,1,0:T(8,128)}, u32[]{:S(2)}, u32[]{:S(2)}) collective-permute-start(f32[2,192,256]{2,1,0:T(8,128)} %get-tuple-element.31), channel_id=1, source_target_pairs={{0,4},{1,5},{2,6},{3,7},{4,0},{5,1},{6,2},{7,3},{8,12},{9,13},{10,... | collective-permute-start | bytes 1179656 | tf_op jit(solution)/shard_map/ppermute | solution.py:358
  145.5 22.8 %collective-permute-start.18 = (f32[2,192,256]{2,1,0:T(8,128)}, f32[2,192,256]{2,1,0:T(8,128)}, u32[]{:S(2)}, u32[]{:S(2)}) collective-permute-start(f32[2,192,256]{2,1,0:T(8,128)} %get-tuple-element.32), channel_id=1, source_target_pairs={{0,6},{1,7},{2,4},{3,5},{4,2},{5,3},{6,0},{7,1},{8,14},{9,15},{10,... | collective-permute-start | bytes 1179656 | tf_op jit(solution)/shard_map/ppermute | solution.py:358
  149.5 24.8 %collective-permute-start.34 = (f32[384,128]{1,0:T(8,128)S(1)}, f32[384,128]{1,0:T(8,128)}, u32[]{:S(2)}, u32[]{:S(2)}) collective-permute-start(f32[384,128]{1,0:T(8,128)S(1)} %shard_map.74.refs_4_), channel_id=1, source_target_pairs={{0,2},{1,3},{2,0},{3,1},{4,6},{5,7},{6,4},{7,5},{8,10},{9,11},{10,... | collective-permute-start | bytes 589832 | tf_op jit(solution)/shard_map/ppermute | solution.py:358
  149.6 0.7 copy-start.14
  150.3 28.4 %collective-permute-start.35 = (f32[384,128]{1,0:T(8,128)S(1)}, f32[384,128]{1,0:T(8,128)}, u32[]{:S(2)}, u32[]{:S(2)}) collective-permute-start(f32[384,128]{1,0:T(8,128)S(1)} %shard_map.74.refs_4_), channel_id=1, source_target_pairs={{0,4},{1,5},{2,6},{3,7},{4,0},{5,1},{6,2},{7,3},{8,12},{9,13},{10,... | collective-permute-start | bytes 589832 | tf_op jit(solution)/shard_map/ppermute | solution.py:358
  152.8 0.7 copy-start.10
  153.6 25.5 %collective-permute-start.36 = (f32[384,128]{1,0:T(8,128)S(1)}, f32[384,128]{1,0:T(8,128)}, u32[]{:S(2)}, u32[]{:S(2)}) collective-permute-start(f32[384,128]{1,0:T(8,128)S(1)} %shard_map.74.refs_4_), channel_id=1, source_target_pairs={{0,6},{1,7},{2,4},{3,5},{4,2},{5,3},{6,0},{7,1},{8,14},{9,15},{10,... | collective-permute-start | bytes 589832 | tf_op jit(solution)/shard_map/ppermute | solution.py:358
  168.3 1.0 copy-start.9
  169.3 1.0 copy-start.11
  170.3 0.9 copy-start.13
  171.2 0.9 copy-start.15
  173.4 10.8 %collective-permute-start.20 = (f32[192,256]{1,0:T(8,128)S(1)}, f32[192,256]{1,0:T(8,128)S(1)}, u32[]{:S(2)}, u32[]{:S(2)}) collective-permute-start(f32[192,256]{1,0:T(8,128)S(1)} %get-tuple-element.36), channel_id=1, source_target_pairs={{0,1},{1,0},{2,3},{3,2},{4,5},{5,4},{6,7},{7,6},{8,9},{9,8},{10,11... | collective-permute-start | bytes 589832 | tf_op jit(solution)/shard_map/ppermute | solution.py:358
  174.3 8.6 %collective-permute-start.21 = (f32[64,256]{1,0:T(8,128)S(1)}, f32[64,256]{1,0:T(8,128)S(1)}, u32[]{:S(2)}, u32[]{:S(2)}) collective-permute-start(f32[64,256]{1,0:T(8,128)S(1)} %get-tuple-element.38), channel_id=1, source_target_pairs={{0,2},{1,3},{2,0},{3,1},{4,6},{5,7},{6,4},{7,5},{8,10},{9,11},{10,... | collective-permute-start | bytes 196616 | tf_op jit(solution)/shard_map/ppermute | solution.py:358
  174.3 8.6 %collective-permute-start.22 = (f32[64,256]{1,0:T(8,128)S(1)}, f32[64,256]{1,0:T(8,128)S(1)}, u32[]{:S(2)}, u32[]{:S(2)}) collective-permute-start(f32[64,256]{1,0:T(8,128)S(1)} %get-tuple-element.39), channel_id=1, source_target_pairs={{0,4},{1,5},{2,6},{3,7},{4,0},{5,1},{6,2},{7,3},{8,12},{9,13},{10,... | collective-permute-start | bytes 196616 | tf_op jit(solution)/shard_map/ppermute | solution.py:358
  178.7 5.5 %collective-permute-start.23 = (f32[64,256]{1,0:T(8,128)S(1)}, f32[64,256]{1,0:T(8,128)S(1)}, u32[]{:S(2)}, u32[]{:S(2)}) collective-permute-start(f32[64,256]{1,0:T(8,128)S(1)} %get-tuple-element.40), channel_id=1, source_target_pairs={{0,6},{1,7},{2,4},{3,5},{4,2},{5,3},{6,0},{7,1},{8,14},{9,15},{10,... | collective-permute-start | bytes 196616 | tf_op jit(solution)/shard_map/ppermute | solution.py:358
  180.1 20.0 %collective-permute-start.37 = (f32[256,128]{1,0:T(8,128)S(1)}, f32[256,128]{1,0:T(8,128)S(1)}, u32[]{:S(2)}, u32[]{:S(2)}) collective-permute-start(f32[256,128]{1,0:T(8,128)S(1)} %fusion.refs_8_), channel_id=1, source_target_pairs={{0,1},{1,0},{2,3},{3,2},{4,5},{5,4},{6,7},{7,6},{8,9},{9,8},{10,11... | collective-permute-start | bytes 393224 | tf_op jit(solution)/shard_map/ppermute | solution.py:358
  184.2 22.2 %copy-start.5 = (f32[256,128]{1,0:T(8,128)S(1)}, f32[256,128]{1,0:T(8,128)}, u32[]{:S(2)}) copy-start(f32[256,128]{1,0:T(8,128)} %copy-done.3) | copy-start | bytes 393220
  184.9 15.2 %collective-permute-start.24 = (bf16[256,256]{1,0:T(8,128)(2,1)S(1)}, bf16[256,256]{1,0:T(8,128)(2,1)S(1)}, u32[]{:S(2)}, u32[]{:S(2)}) collective-permute-start(bf16[256,256]{1,0:T(8,128)(2,1)S(1)} %get-tuple-element.41), channel_id=1, source_target_pairs={{1,112},{4,116},{0,16},{5,4},{2,19},{6,131},{3,117},{7,125},{9,120... | collective-permute-start | bytes 393224 | tf_op jit(solution)/shard_map/ppermute | solution.py:451
  189.4 10.7 %collective-permute-start.25 = (bf16[256,256]{1,0:T(8,128)(2,1)S(1)}, bf16[256,256]{1,0:T(8,128)(2,1)S(1)}, u32[]{:S(2)}, u32[]{:S(2)}) collective-permute-start(bf16[256,256]{1,0:T(8,128)(2,1)S(1)} %get-tuple-element.42), channel_id=1, source_target_pairs={{1,19},{4,131},{2,124},{0,0},{6,8},{5,128},{3,163},{10,104},{8,27}... | collective-permute-start | bytes 393224 | tf_op jit(solution)/shard_map/ppermute | solution.py:451
  195.5 4.6 %collective-permute-start.26 = (bf16[256,256]{1,0:T(8,128)(2,1)S(1)}, bf16[256,256]{1,0:T(8,128)(2,1)S(1)}, u32[]{:S(2)}, u32[]{:S(2)}) collective-permute-start(bf16[256,256]{1,0:T(8,128)(2,1)S(1)} %get-tuple-element.43), channel_id=1, source_target_pairs={{3,120},{2,96},{0,19},{4,131},{6,108},{1,35},{7,163},{5,101},{11,2... | collective-permute-start | bytes 393224 | tf_op jit(solution)/shard_map/ppermute | solution.py:451
  197.4 9.0 %collective-permute-start.27 = (bf16[256,256]{1,0:T(8,128)(2,1)S(1)}, bf16[256,256]{1,0:T(8,128)(2,1)S(1)}, u32[]{:S(2)}, u32[]{:S(2)}) collective-permute-start(bf16[256,256]{1,0:T(8,128)(2,1)S(1)} %get-tuple-element.44), channel_id=1, source_target_pairs={{3,19},{2,131},{6,16},{7,8},{0,104},{4,100},{1,97},{5,163},{9,27},... | collective-permute-start | bytes 393224 | tf_op jit(solution)/shard_map/ppermute | solution.py:451
where the time goes:
time: 212 us; the launch traced here: 209 us
  starting transfers between devices  89.8 us (42%)
  waiting for transfers between devices  77.2 us (36%)
  Pallas kernels  20.8 us (10%)
  local copies, waits for them, and re-layouts  13 us (6%)
  other arithmetic  5.19 us (2%)
    ppermute x14, waiting for transfers between devices, move(): return lax.ppermute(x, 'dp', perm)  50.1 us
    ppermute x20, starting transfers between devices, from_feat(): return lax.ppermute(x, 'feat', [(f, f ^ s) for f in range(NF)])  35.1 us
    all_to_all x2, starting transfers between devices, exchange(): lax.all_to_all(value, axis, split_axis=0, concat_axis=0, tiled=True, axis...  23.1 us
    pallas_call x8, Pallas kernels, call(): pl.pallas_call(kernel, in_specs=[pl.BlockSpec(memory_space=pltpu.SMEM)] *...  20.8 us
    ppermute x20, waiting for transfers between devices, from_feat(): return lax.ppermute(x, 'feat', [(f, f ^ s) for f in range(NF)])  20.8 us
    ppermute x14, starting transfers between devices, move(): return lax.ppermute(x, 'dp', perm)  17.2 us
    ppermute x4, starting transfers between devices, body(): got.append(lax.ppermute(out[c], ('dp', 'feat'), perms[c]))  14.4 us
    unnamed x36, local copies, waits for them, and re-layouts  8.92 us
  transfers between devices with their start and end apart: 40, of which 15 were waited for; matrix products, arithmetic and copies ran while one was open for 5% of the time, Pallas kernels for 9%

commit v1 on v0

--- a/solution.py
+++ b/solution.py
@@ -91,32 +91,77 @@
     return colour
 
 
-def hops(a, z, f, i, g):
-    steps = ((f % 2 * 2 + a - g % 2 * 2 - i // (2 * NZ), 4), (f // 2 - g // 2, 4), (z - i // 2, NZ))
-    return sum(min(d % n, -d % n) for d, n in steps)
+SIZES = (2 * 2, NF // 2, NZ)
+
+
+def chip(i, f):
+    return f % 2 * 2 + i // (2 * NZ), f // 2, i // 2 % NZ
+
+
+def links(src, dst, memo):
+    if (src, dst) not in memo:
+        at, part = [], []
+        for k, axes in enumerate(((2, 1, 0), (2, 0, 1))):
+            here = list(src)
+            for axis in axes:
+                n = SIZES[axis]
+                ahead = (dst[axis] - here[axis]) % n
+                ways = [(1, ahead), (-1, n - ahead)]
+                short = [w for w in ways if w[1] == min(ahead, n - ahead)]
+                for sign, steps in short:
+                    now = list(here)
+                    for _ in range(steps):
+                        at.append(np.ravel_multi_index((k, axis, (1 + sign) // 2, *now), (2, 3, 2, *SIZES)))
+                        part.append(1.0 / len(short))
+                        now[axis] = (now[axis] + sign) % n
+                here[axis] = dst[axis]
+        memo[src, dst] = np.array(at, np.int64), np.array(part)
+    return memo[src, dst]
 
 
 def reducers():
     per = len(PLACES) // NF
-    table = np.zeros((len(PLACES), 2, NF), np.int32)
-    for a, z, k in PLACES:
-        for round_, pairs in enumerate(pair_lists(a, z, k)):
-            cost = [
-                [
-                    hops(a, z, f, r, c // per) ** 3 + hops(a, z, f, c, r // per) ** 3
-                    for f in range(NF)
-                ]
-                for r, c in pairs
-            ]
-            at, better = list(range(NF)), True
-            while better:
-                better = False
+    table = np.tile(np.arange(NF, dtype=np.int32), (len(PLACES), 2, 1))
+    memo, load, owners, far = {}, np.zeros(2 * 3 * 2 * len(PLACES) * NF // 2), {}, {}
+    for p in PLACES:
+        i = row_block(*p)
+        for round_, pairs in enumerate(pair_lists(*p)):
+            for slot, (r, c) in enumerate(pairs):
+                ends = [chip(r, c // per), chip(c, r // per)][: 1 if (round_, slot) == (0, 6) else 2]
+                owners[i, round_, slot] = ends
+                for f in range(NF):
+                    hops = [
+                        sum(min((x - y) % n, (y - x) % n) for x, y, n in zip(chip(i, f), dst, SIZES))
+                        for dst in ends
+                    ]
+                    far[i, round_, slot, f] = 30 * sum(h**3 for h in hops)
+
+    def put(key, f, weight):
+        for dst in owners[key]:
+            at, part = links(chip(key[0], f), dst, memo)
+            np.add.at(load, at, weight * part)
+
+    def swap(a, b, f, g):
+        for key, old, new in ((a, f, g), (b, g, f)):
+            put(key, old, -1)
+            put(key, new, 1)
+
+    for key in owners:
+        put(key, int(table[key]), 1)
+    for sweep in range(10):
+        power = 4 if sweep >= 3 else 0
+        for i in range(len(PLACES)):
+            for round_ in range(2):
                 for p in range(NF):
                     for q in range(p):
-                        now = cost[p][at[p]] + cost[q][at[q]]
-                        if cost[p][at[q]] + cost[q][at[p]] < now:
-                            at[p], at[q], better = at[q], at[p], True
-            table[row_block(a, z, k), round_] = at
+                        a, b = (i, round_, p), (i, round_, q)
+                        f, g = int(table[a]), int(table[b])
+                        before = (load**power).sum() + far[(*a, f)] + far[(*b, g)]
+                        swap(a, b, f, g)
+                        if (load**power).sum() + far[(*a, g)] + far[(*b, f)] < before - 1e-6:
+                            table[a], table[b] = g, f
+                        else:
+                            swap(a, b, g, f)
     return table
 
 
@@ -149,6 +194,21 @@
     return perms, sends, takes
 
 
+COLUMN_0, LOW_HALF, CORE, Y, AT, SENDS, TAKES = 0, 1, 2, 3, 4, 4 + 2 * NF, 8 + 2 * NF
+
+
+def facts(table, sends, takes):
+    rows = np.zeros((len(PLACES) * NF, 12 + 2 * NF), np.int32)
+    for a, z, k in PLACES:
+        i = row_block(a, z, k)
+        for f in range(NF):
+            at = table[i] ^ f
+            rows[i * NF + f] = [
+                a == 0, z < NZ // 2, k, f // 2, *at[0], *at[1], *sends[i * NF + f], *takes[i * NF + f]
+            ]
+    return rows
+
+
 def exchange(value, axis, groups=None):
     return lax.all_to_all(
         value, axis, split_axis=0, concat_axis=0, tiled=True, axis_index_groups=groups
@@ -168,7 +228,7 @@
     return (y[:, 2 * q :] + y[:, q : 2 * q]) + y[:, :q]
 
 
-def hdot_kernel(core, own, part, part_, first, mine, other):
+def hdot_kernel(info, own, part, part_, first, mine, other):
     value = part[...] + part_[...]
     first[...] = value
     terms = parts_of(value)
@@ -183,20 +243,20 @@
             )
         )
 
-        @pl.when(core[0] == at)
+        @pl.when(info[CORE] == at)
         def _():
             mine[...] = rows
 
-        @pl.when(core[0] != at)
+        @pl.when(info[CORE] != at)
         def _():
             other[...] = rows
 
 
-def gdot_kernel(core, own, mine, other, first, one, one_, out):
+def gdot_kernel(info, own, mine, other, first, one, one_, out):
     half = mine.shape[0]
     total = None
     for at in range(2):
-        back = jnp.where(core[0] == at, mine[...], other[...])
+        back = jnp.where(info[CORE] == at, mine[...], other[...])
         term = three(
             jnp.dot(
                 own[:, at * half : (at + 1) * half], parts_of(back), preferred_element_type=jnp.float32
@@ -206,7 +266,7 @@
     wide = own[...].astype(jnp.float32)
     rows, q = first.shape
     out[:rows] = total - jnp.sum(wide * wide, axis=1, keepdims=True) * first[...]
-    square = one[2 * rows :] + one_[rows:]
+    square = one[rows:] + one_[rows:]
     piece = square.shape[0]
     out[rows : rows + piece] = square[:, :q]
     out[rows + piece :] = square[:, q:]
@@ -218,11 +278,11 @@
     )
 
 
-def products(plan, ins, flags):
+def products(plan, ins, info):
     for left, right in plan:
         if isinstance(left, tuple):
             i, j, flag = left
-            value = jnp.where(flags[flag] > 0, ins[i][...], ins[j][...])
+            value = jnp.where(info[flag] > 0, ins[i][...], ins[j][...])
         else:
             value = ins[left][...]
         if isinstance(right, tuple):
@@ -233,16 +293,16 @@
 
 
 UP = (4, 5)
-PLAN_1 = ((0, UP), (1, UP), (2, UP), (3, UP), (0, 6), (1, 6), ((2, 3, 0), 6), (3, 2))
+PLAN_1 = ((0, UP), (1, UP), (2, UP), (3, UP), (0, 6), (1, 6), ((2, 3, COLUMN_0), 6), (3, 2))
 SLOTS_1 = (0, 1, 4, 5, 2, 3, 7, 6)
 PLAN_2A = ((0, (2, 3)), (1, (2, 3)), (0, 4), (1, 4))
-PLAN_2B = (((0, 1, 1), (4, 5)), (2, (6, 7)), (3, (6, 7)), ((0, 1, 0), (6, 7)))
-
-
-def kernel_1(flags, order, y, *refs):
+PLAN_2B = (((0, 1, LOW_HALF), (4, 5)), (2, (6, 7)), (3, (6, 7)), ((0, 1, COLUMN_0), (6, 7)))
+
+
+def kernel_1(info, *refs):
     ins, outs, acc = refs[:7], refs[7:11], refs[11]
-    for slot, product in zip(SLOTS_1, products(PLAN_1, ins, flags)):
-        acc[order[0, slot]] = product
+    for slot, product in zip(SLOTS_1, products(PLAN_1, ins, info)):
+        acc[info[AT + slot]] = product
     square = tile(ins[2][...], ins[2][...])
     rows = square.shape[0]
     own = lax.broadcasted_iota(jnp.int32, (rows, rows), 0)
@@ -252,49 +312,41 @@
     for dy, out in enumerate(outs):
         out[:rows] = acc[2 * dy]
         out[rows : 2 * rows] = acc[2 * dy + 1]
-        at = pl.multiple_of((y[0] ^ dy) * piece, piece)
+        at = pl.multiple_of((info[Y] ^ dy) * piece, piece)
         out[2 * rows :] = acc[NF, pl.ds(at, piece)]
 
 
-def kernel_2a(flags, *refs):
-    for slot, product in enumerate(products(PLAN_2A, refs[:5], flags)):
+def kernel_2a(info, *refs):
+    for slot, product in enumerate(products(PLAN_2A, refs[:5], info)):
         refs[5][slot] = product
 
 
-def kernel_2b(flags, order, *refs):
+def kernel_2b(info, *refs):
     ins, early, along_y, along_x, acc = refs[:8], refs[8], refs[9:13], refs[13:15], refs[15]
-    for slot, product in enumerate(products(PLAN_2B, ins, flags)):
-        acc[order[1, NF // 2 + slot]] = product
+    for slot, product in enumerate(products(PLAN_2B, ins, info)):
+        acc[info[AT + NF + NF // 2 + slot]] = product
     for slot in range(NF // 2):
-        acc[order[1, slot]] = early[slot]
+        acc[info[AT + NF + slot]] = early[slot]
     cut = along_y[0].shape[1]
     for s in range(NF):
         along_y[s // 2][s % 2] = acc[s, :cut]
         along_x[s % 2][s // 2] = acc[s, cut:]
 
 
-def mid_kernel(a, b, c, d, low, low_, keep, send, *lowers):
-    upper = (a[...] + b[...]) + (c[...] + d[...])
-    keep[...] = upper[0]
-    send[...] = upper[1]
-    for dy, out in enumerate(lowers):
-        out[...] = low[dy] + low_[dy]
-
-
-def items_kernel(sends, one_ref, one_ref_, up, up_, a, b, c, d, *outs):
+def items_kernel(info, one_ref, one_ref_, up, up_, a, b, c, d, *outs):
     rows = one_ref.shape[1]
-    one = one_ref[:rows] + one_ref_[:rows]
+    one = one_ref[...] + one_ref_[:rows]
     lower = (a[...] + b[...]) + (c[...] + d[...])
     two = jnp.concatenate([up[...] + up_[...], lower], axis=0)
     choices = [x.astype(jnp.bfloat16) for x in (one, one.T, two, two.T)]
     for n, out in enumerate(outs):
         value = choices[3]
         for q in (2, 1, 0):
-            value = jnp.where(sends[n] == q, choices[q], value)
+            value = jnp.where(info[SENDS + n] == q, choices[q], value)
         out[...] = value
 
 
-def place_kernel(weight, takes, y, *refs):
+def place_kernel(weight, info, *refs):
     got, pieces, (total, total_, first), (out, scores), diagonal = (
         refs[:4], refs[4:8], refs[8:11], refs[11:13], refs[13]
     )
@@ -302,30 +354,30 @@
     piece = 2 * rows // NF
     half = first.shape[1]
     for dy, source in enumerate(pieces):
-        at = pl.multiple_of((y[0] ^ dy) * piece, piece)
+        at = pl.multiple_of((info[Y] ^ dy) * piece, piece)
         diagonal[pl.ds(at, piece), :half] = source[rows : rows + piece].astype(jnp.bfloat16)
         diagonal[pl.ds(at, piece), half:] = source[rows + piece :].astype(jnp.bfloat16)
     values = [x[...] for x in got]
     for s in range(4):
         value = diagonal[...]
         for q in range(4):
-            value = jnp.where(takes[s] == q, values[q], value)
+            value = jnp.where(info[TAKES + s] == q, values[q], value)
         out[:, s * rows : (s + 1) * rows] = value
     scores[...] = first[...] - weight * (total[...] + total_[...])
 
 
-def call(kernel, scalars, operands, outs, scratch=(), flops=0):
+def call(kernel, info, operands, outs, scratch=(), flops=0):
     vmem = pl.BlockSpec(memory_space=pltpu.VMEM)
     moved = sum(x.size * x.dtype.itemsize for x in (*operands, *outs))
     return pl.pallas_call(
         kernel,
-        in_specs=[pl.BlockSpec(memory_space=pltpu.SMEM)] * len(scalars) + [vmem] * len(operands),
+        in_specs=[pl.BlockSpec(memory_space=pltpu.SMEM)] + [vmem] * len(operands),
         out_specs=[vmem] * len(outs),
         out_shape=list(outs),
         scratch_shapes=list(scratch),
         compiler_params=pltpu.CompilerParams(vmem_limit_bytes=24 * 2**20),
         cost_estimate=pl.CostEstimate(flops=flops, bytes_accessed=moved, transcendentals=0),
-    )(*scalars, *operands)
+    )(info, *operands)
 
 
 def array(dtype, *shape):
@@ -338,17 +390,8 @@
     tile_flops = 2 * rows * rows * depth
     table = reducers()
     perms, sends, takes = routes(table)
-    dp = lax.axis_index("dp")
-    feat = lax.axis_index("feat")
-    me = dp * NF + feat
-    column_0 = dp < 2 * NZ
-    low_half = (dp // 2) % NZ < NZ // 2
-    core = dp % 2
-    flags = jnp.stack([column_0, low_half]).astype(jnp.int32)
-    order = jnp.asarray(table)[dp] ^ feat
-    y = feat // 2
-    send = jnp.asarray(sends)[me]
-    take = jnp.asarray(takes)[me]
+    me = lax.axis_index("dp") * NF + lax.axis_index("feat")
+    info = jnp.asarray(facts(table, sends, takes))[me]
     f32, bf16 = jnp.float32, jnp.bfloat16
 
     def move(x, perm):
@@ -373,49 +416,54 @@
     first, _ = over_y([first] * 4)
     first_ = from_feat(first, 1)
 
-    high = 3 * rows // 4
+    high = 5 * rows // 8
     up2 = [move(up1[0], FROM_ABOVE), move(up1[1], FROM_ABOVE)]
     down2 = move(down1, FROM_BELOW)
     down1_ = move(down1, OTHER_CORE)
 
     one = call(
         kernel_1,
-        (flags, order, y[None]),
+        info,
         (down1, down1_, own, own_, *up1, side),
         [array(f32, 2 * rows + 2 * rows // NF, rows)] * 4,
         [pltpu.VMEM((NF + 1, rows, rows), f32)],
         (NF + 1) * tile_flops,
     )
-    one, _ = over_y(one)
+    parts = [one[0]] + [from_feat(one[dy], 2 * dy) for dy in (1, 2, 3)]
+    one, send_ = (
+        (a + b) + (c + d) for a, b, c, d in ([p[:rows] for p in parts], [p[rows:] for p in parts])
+    )
 
     half = depth // 2
     q = first.shape[1]
     first, mine, other = call(
         hdot_kernel,
-        (core[None],),
+        info,
         (own, first, first_),
         [array(f32, rows, q), array(f32, half, q), array(f32, half, q)],
         flops=6 * rows * depth * q,
     )
-    mine = mine + move(other, OTHER_CORE)
+    other = move(other, OTHER_CORE)
+    mine = mine + other
+    far = [move(up2[0], OTHER_COLUMN), move(up2[1], OTHER_COLUMN)]
+    mine, far[0] = lax.optimization_barrier((mine, far[0]))
     chips = 2 * NZ
     mine = exchange(mine.reshape(chips, -1, mine.shape[1]), "dp", CHIP_GROUPS)
     mine = mine.sum(axis=0)
     mine = exchange(jnp.broadcast_to(mine, (chips, *mine.shape)), "dp", CHIP_GROUPS)
     mine = mine.reshape(half, -1)
 
-    far = [move(up2[0], OTHER_COLUMN), move(up2[1], OTHER_COLUMN)]
     down2_ = move(down2, OTHER_CORE)
     (early,) = call(
         kernel_2a,
-        (flags,),
+        info,
         (down2, down2_, *up1, side),
         [array(f32, NF // 2, rows, rows)],
         flops=4 * tile_flops,
     )
     two = call(
         kernel_2b,
-        (flags, order),
+        info,
         (down2, down2_, down1, down1_, *up2, *far, early),
         [array(f32, 2, high, rows)] * 4 + [array(f32, 4, rows - high, rows)] * 2,
         [pltpu.VMEM((NF, rows, rows), f32)],
@@ -423,36 +471,34 @@
     )
     upper = [two[0]] + [from_feat(two[dy], 2 * dy) for dy in (1, 2, 3)]
     lower_ = from_feat(two[5], 1)
-    one_ = from_feat(one[rows:], 1)
+    one_ = from_feat(send_, 1)
+    one_part = send_
     piece = 2 * rows // NF
-    upper, send_, *lower = call(
-        mid_kernel,
-        (),
-        (*upper, two[4], lower_),
-        [array(f32, high, rows)] * 2 + [array(f32, rows - high, rows)] * 4,
-    )
+    upper = (upper[0] + upper[1]) + (upper[2] + upper[3])
+    lower = [two[4][dy] + lower_[dy] for dy in range(4)]
+    upper, send_ = upper[0], upper[1]
     upper_ = from_feat(send_, 1)
     lower = [lower[0]] + [from_feat(lower[dy], 2 * dy) for dy in (1, 2, 3)]
 
     other = move(mine, OTHER_CORE)
     (shared,) = call(
         gdot_kernel,
-        (core[None],),
-        (own, mine, other, first, one, one_),
+        info,
+        (own, mine, other, first, one_part, one_),
         [array(f32, rows + 2 * piece, q)],
         flops=6 * rows * depth * q,
     )
     total, pieces = over_y([shared] * 4, rows)
     total_ = from_feat(total, 1)
 
-    out = call(items_kernel, (send,), (one, one_, upper, upper_, *lower), [array(bf16, rows, rows)] * 4)
+    out = call(items_kernel, info, (one, one_, upper, upper_, *lower), [array(bf16, rows, rows)] * 4)
     got = []
     for c in range(4):
         got.append(lax.ppermute(out[c], ("dp", "feat"), perms[c]))
     return tuple(
         call(
             functools.partial(place_kernel, pair_weight),
-            (take, y[None]),
+            info,
             (*got, *pieces, total, total_, first),
             [array(bf16, rows, 4 * rows), array(f32, rows, q)],
             [pltpu.VMEM((rows, rows), bf16)],

time: 212 us -> 186 us (0.88)
  starting transfers between devices: 89.8 us -> 79.5 us
  waiting for transfers between devices: 77.2 us -> 70.3 us
  local copies, waits for them, and re-layouts: 13 us -> 6.44 us
    all_to_all x2, starting transfers between devices: 23.1 us -> 16 us  [exchange(): lax.all_to_all(value, axis, split_axis=0, concat_axis=0, tiled=True, axis...]
    ppermute x14, waiting for transfers between devices: 50.1 us -> 43 us  [move(): return lax.ppermute(x, 'dp', perm)]
    unnamed x36 -> x20, local copies, waits for them, and re-layouts: 8.92 us -> 2.68 us
    ppermute x14, starting transfers between devices: 17.2 us -> 13.1 us  [move(): return lax.ppermute(x, 'dp', perm)]
    add x1 -> x5, other arithmetic: 0.87 us -> 4.61 us  [the longest x2 2.53 us: body(): a + b + (c + d)]
    ppermute x20, waiting for transfers between devices: 20.8 us -> 24.1 us  [from_feat(): return lax.ppermute(x, 'feat', [(f, f ^ s) for f in range(NF)])]
    ppermute x4, waiting for transfers between devices: 6.32 us -> 3.07 us  [body(): got.append(lax.ppermute(out[c], ('dp', 'feat'), perms[c]))]
    add x3 -> x2, other arithmetic: 2.48 us -> 0.06 us  [over_y(): return (a + b + (c + d), parts)]
  transfers between devices with their start and end apart: 40 -> 40, of which waited for: 15 -> 14; matrix products, arithmetic and copies ran while one was open for 5% -> 4% of each run, Pallas kernels for 9% -> 10%
where the time goes in v1:
time: 186 us; the launch traced here: 183 us
  starting transfers between devices  79.5 us (43%)
  waiting for transfers between devices  70.3 us (38%)
  Pallas kernels  19.4 us (10%)
  local copies, waits for them, and re-layouts  6.44 us (3%)
  other arithmetic  5.75 us (3%)
    ppermute x14, waiting for transfers between devices, move(): return lax.ppermute(x, 'dp', perm)  43 us
    ppermute x20, starting transfers between devices, from_feat(): return lax.ppermute(x, 'feat', [(f, f ^ s) for f in range(NF)])  34.7 us
    ppermute x20, waiting for transfers between devices, from_feat(): return lax.ppermute(x, 'feat', [(f, f ^ s) for f in range(NF)])  24.1 us
    pallas_call x7, Pallas kernels, call(): pl.pallas_call(kernel, in_specs=[pl.BlockSpec(memory_space=pltpu.SMEM)] +...  19.4 us
    all_to_all x2, starting transfers between devices, exchange(): lax.all_to_all(value, axis, split_axis=0, concat_axis=0, tiled=True, axis...  16 us
    ppermute x4, starting transfers between devices, body(): got.append(lax.ppermute(out[c], ('dp', 'feat'), perms[c]))  15.7 us
    ppermute x14, starting transfers between devices, move(): return lax.ppermute(x, 'dp', perm)  13.1 us
  transfers between devices with their start and end apart: 40, of which 14 were waited for; matrix products, arithmetic and copies ran while one was open for 4% of the time, Pallas kernels for 10%

profile of v1, /device:TPU:32, one launch (start us, length us, event | category | flops | bytes accessed | tf_op | source)
XLA Modules:
  0.0 182.8 jit_solution(15276350310352152726)
XLA Ops:
  0.7 2.2 %fusion.7 = (bf16[128,2048]{1,0:T(8,128)(2,1)}, bf16[128,2048]{1,0:T(8,128)(2,1)S(1)}) fusion(bf16[256,2048]{1,0:T(8,128)(2,1)} %own.3), kind=kLoop, calls=%fused_computation.22 | loop fusion | bytes 2097152 | tf_op jit(solution)/shard_map/slice | solution.py:410
  2.9 1.8 collective-permute-start.3
  4.9 0.4 fusion.8
  5.3 3.3 %collective-permute-start.15 = (f32[256,128]{1,0:T(8,128)S(1)}, f32[256,128]{1,0:T(8,128)S(1)}, u32[]{:S(2)}, u32[]{:S(2)}) collective-permute-start(f32[256,128]{1,0:T(8,128)S(1)} %fusion.8), channel_id=1, source_target_pairs={{0,4},{1,5},{2,6},{3,7},{4,0},{5,1},{6,2},{7,3},{8,12},{9,13},{10,... | collective-permute-start | bytes 393224 | tf_op jit(solution)/shard_map/ppermute | solution.py:401
  8.6 1.1 collective-permute-start.16
  9.7 7.0 %collective-permute-done.3.refs_4_.refs_2_ = bf16[128,2048]{1,0:T(8,128)(2,1)S(1)} collective-permute-done((bf16[128,2048]{1,0:T(8,128)(2,1)S(1)}, bf16[128,2048]{1,0:T(8,128)(2,1)S(1)}, u32[]{:S(2)}, u32[]{:S(2)}) %collective-permute-start.3) | collective-permute-done | bytes 524320 | tf_op jit(solution)/shard_map/ppermute | solution.py:398
  16.7 3.3 %collective-permute-start.12 = (bf16[128,2048]{1,0:T(8,128)(2,1)S(1)}, bf16[128,2048]{1,0:T(8,128)(2,1)}, u32[]{:S(2)}, u32[]{:S(2)}) collective-permute-start(bf16[128,2048]{1,0:T(8,128)(2,1)S(1)} %collective-permute-done.3.refs_4_.refs_2_), channel_id=1, source_target_pairs={{0,112},{8,120},{16,0},{24,8},{32,16},{40,24},{48,32},{56,40},{64,... | collective-permute-start | bytes 1572872 | tf_op jit(solution)/shard_map/ppermute | solution.py:398
  20.1 3.1 %collective-permute-start.17 = (f32[256,128]{1,0:T(8,128)S(1)}, f32[256,128]{1,0:T(8,128)S(1)}, u32[]{:S(2)}, u32[]{:S(2)}) collective-permute-start(f32[256,128]{1,0:T(8,128)S(1)} %add_add_fusion.1.part), channel_id=1, source_target_pairs={{0,1},{1,0},{2,3},{3,2},{4,5},{5,4},{6,7},{7,6},{8,9},{9,8},{10,11... | collective-permute-start | bytes 393224 | tf_op jit(solution)/shard_map/ppermute | solution.py:401
  23.2 0.7 dynamic-slice_bitcast_fusion.info
  23.9 2.8 %collective-permute-done.17.part_ = f32[256,128]{1,0:T(8,128)S(1)} collective-permute-done((f32[256,128]{1,0:T(8,128)S(1)}, f32[256,128]{1,0:T(8,128)S(1)}, u32[]{:S(2)}, u32[]{:S(2)}) %collective-permute-start.17) | collective-permute-done | bytes 131104 | tf_op jit(solution)/shard_map/ppermute | solution.py:401
  26.6 1.5 shard_map.51
  28.3 2.1 %collective-permute-done.12.refs_4_ = bf16[128,2048]{1,0:T(8,128)(2,1)} collective-permute-done((bf16[128,2048]{1,0:T(8,128)(2,1)S(1)}, bf16[128,2048]{1,0:T(8,128)(2,1)}, u32[]{:S(2)}, u32[]{:S(2)}) %collective-permute-start.12) | collective-permute-done | bytes 524320 | tf_op jit(solution)/shard_map/ppermute | solution.py:398
  30.3 1.5 collective-permute-start.19
  31.8 2.7 %collective-permute-start.10 = (bf16[256,2048]{1,0:T(8,128)(2,1)}, bf16[256,2048]{1,0:T(8,128)(2,1)S(1)}, u32[]{:S(2)}, u32[]{:S(2)}) collective-permute-start(bf16[256,2048]{1,0:T(8,128)(2,1)} %collective-permute-done.refs_0_.refs_2_), channel_id=1, source_target_pairs={{0,16},{8,24},{16,32},{24,40},{32,48},{40,56},{48,64},{56,72},{64,... | collective-permute-start | bytes 3145736 | tf_op jit(solution)/shard_map/ppermute | solution.py:398
  34.6 0.9 collective-permute-start.4
  35.5 0.7 collective-permute-start.5
  36.3 9.1 %collective-permute-done.19.refs_6_ = bf16[128,2048]{1,0:T(8,128)(2,1)S(1)} collective-permute-done((bf16[128,2048]{1,0:T(8,128)(2,1)}, bf16[128,2048]{1,0:T(8,128)(2,1)S(1)}, u32[]{:S(2)}, u32[]{:S(2)}) %collective-permute-start.19) | collective-permute-done | bytes 524320 | tf_op jit(solution)/shard_map/ppermute | solution.py:398
  45.3 0.8 copy-done.6
  46.1 0.9 add.88
  47.1 9.7 %all-to-all-start = ((f32[16,64,128]{2,1,0:T(8,128)}), f32[16,64,128]{2,1,0:T(8,128)}, u32[]{:S(2)}, u32[]{:S(2)}) async-start(f32[16,64,128]{2,1,0:T(8,128)} %bitcast.20), calls=%async_computation | async-start | bytes 1048576 | tf_op jit(solution)/shard_map/all_to_all | solution.py:213
  57.2 24.6 %collective-permute-done.13.refs_5_ = bf16[128,2048]{1,0:T(8,128)(2,1)} collective-permute-done((bf16[128,2048]{1,0:T(8,128)(2,1)}, bf16[128,2048]{1,0:T(8,128)(2,1)}, u32[]{:S(2)}, u32[]{:S(2)}) %collective-permute-start.13) | collective-permute-done | bytes 524320 | tf_op jit(solution)/shard_map/ppermute | solution.py:398
  81.8 1.5 collective-permute-start.20
  83.3 6.4 %shard_map.50 = (f32[576,256]{1,0:T(8,128)S(1)}, f32[576,256]{1,0:T(8,128)}, f32[576,256]{1,0:T(8,128)}, f32[576,256]{1,0:T(8,128)}) custom-call(s32[28]{0:T(128)S(1)} %dynamic-slice_bitcast_fusion.info, bf16[256,2048]{1,0:T(8,128)(2,1)} %collective-permute-done.refs_0_.refs_2_, bf16[256,2048]{1,0:T(8,128)(2,1)} %collective-permute-done.1.refs_1_.refs_3_, ...), custom_call_target="tpu_custom_call" | custom-call | flops 2415919104 | bytes 8650752 | tf_op jit(solution)/shard_map/pallas_call | solution.py:372
  89.7 0.8 copy-done.2
  90.5 3.0 %collective-permute-start.8 = (f32[576,256]{1,0:T(8,128)}, f32[576,256]{1,0:T(8,128)}, u32[]{:S(2)}, u32[]{:S(2)}) collective-permute-start(f32[576,256]{1,0:T(8,128)} %get-tuple-element.24), channel_id=1, source_target_pairs={{0,6},{1,7},{2,4},{3,5},{4,2},{5,3},{6,0},{7,1},{8,14},{9,15},{10,... | collective-permute-start | bytes 1769480 | tf_op jit(solution)/shard_map/ppermute | solution.py:401
  93.6 0.6 collective-permute-start.7
  94.2 0.5 collective-permute-start.6
  94.6 1.1 reduce_sum.9
  95.7 0.8 broadcast_in_dim.3
  96.6 6.3 %all-to-all-start.1 = ((f32[16,64,128]{2,1,0:T(8,128)}), f32[16,64,128]{2,1,0:T(8,128)S(1)}, u32[]{:S(2)}, u32[]{:S(2)}) async-start(f32[16,64,128]{2,1,0:T(8,128)} %broadcast_in_dim.3), calls=%async_computation.1 | async-start | bytes 1048576 | tf_op jit(solution)/shard_map/all_to_all | solution.py:213
  102.9 1.0 copy-done.5
  103.9 3.1 %shard_map.52.refs_8_ = f32[4,256,256]{2,1,0:T(8,128)S(1)} custom-call(s32[28]{0:T(128)S(1)} %dynamic-slice_bitcast_fusion.info, bf16[256,2048]{1,0:T(8,128)(2,1)S(1)} %collective-permute-done.10.refs_0_, bf16[256,2048]{1,0:T(8,128)(2,1)} %collective-permute-done.11.refs_1_, bf16[128,2048]{1,0:T(8,128)(2,1)S(1)} %copy-done.5, ...), custom_call_target="tpu_custom_call" | custom-call | flops 1073741824 | bytes 5242880 | tf_op jit(solution)/shard_map/pallas_call | solution.py:372
  107.0 4.8 %shard_map.53 = (f32[2,160,256]{2,1,0:T(8,128)S(1)}, f32[2,160,256]{2,1,0:T(8,128)S(1)}, f32[2,160,256]{2,1,0:T(8,128)S(1)}, f32[2,160,256]{2,1,0:T(8,128)S(1)},...) custom-call(s32[28]{0:T(128)S(1)} %dynamic-slice_bitcast_fusion.info, ...), custom_call_target="tpu_custom_call" | custom-call | flops 1073741824 | bytes 9437184 | tf_op jit(solution)/shard_map/pallas_call | solution.py:372
  111.8 3.2 %collective-permute-start.22 = (f32[2,160,256]{2,1,0:T(8,128)S(1)}, f32[2,160,256]{2,1,0:T(8,128)S(1)}, u32[]{:S(2)}, u32[]{:S(2)}) collective-permute-start(f32[2,160,256]{2,1,0:T(8,128)S(1)} %get-tuple-element.30), channel_id=1, source_target_pairs={{0,4},{1,5},{2,6},{3,7},{4,0},{5,1},{6,2},{7,3},{8,12},{9,13},{10,... | collective-permute-start | bytes 983048 | tf_op jit(solution)/shard_map/ppermute | solution.py:401
  115.0 1.1 collective-permute-start.23
  116.0 5.8 %collective-permute-done.8 = f32[576,256]{1,0:T(8,128)} collective-permute-done((f32[576,256]{1,0:T(8,128)}, f32[576,256]{1,0:T(8,128)}, u32[]{:S(2)}, u32[]{:S(2)}) %collective-permute-start.8) | collective-permute-done | bytes 589856 | tf_op jit(solution)/shard_map/ppermute | solution.py:401
  121.8 0.6 collective-permute-start.21
  122.4 1.3 fusion.one
  123.7 2.8 %collective-permute-start.9 = (f32[320,256]{1,0:T(8,128)S(1)}, f32[320,256]{1,0:T(8,128)S(1)}, u32[]{:S(2)}, u32[]{:S(2)}) collective-permute-start(f32[320,256]{1,0:T(8,128)S(1)} %fusion.one), channel_id=1, source_target_pairs={{0,1},{1,0},{2,3},{3,2},{4,5},{5,4},{6,7},{7,6},{8,9},{9,8},{10,11... | collective-permute-start | bytes 983048 | tf_op jit(solution)/shard_map/ppermute | solution.py:401
  126.5 0.8 collective-permute-start.25
  127.3 3.8 %collective-permute-done.22 = f32[2,160,256]{2,1,0:T(8,128)S(1)} collective-permute-done((f32[2,160,256]{2,1,0:T(8,128)S(1)}, f32[2,160,256]{2,1,0:T(8,128)S(1)}, u32[]{:S(2)}, u32[]{:S(2)}) %collective-permute-start.22) | collective-permute-done | bytes 327712 | tf_op jit(solution)/shard_map/ppermute | solution.py:401
  131.2 1.9 %collective-permute-done.23 = f32[2,160,256]{2,1,0:T(8,128)S(1)} collective-permute-done((f32[2,160,256]{2,1,0:T(8,128)S(1)}, f32[2,160,256]{2,1,0:T(8,128)S(1)}, u32[]{:S(2)}, u32[]{:S(2)}) %collective-permute-start.23) | collective-permute-done | bytes 327712 | tf_op jit(solution)/shard_map/ppermute | solution.py:401
  133.0 0.7 collective-permute-done.21
  133.9 2.8 %collective-permute-start.24 = (f32[160,256]{1,0:T(8,128)S(1)}, f32[160,256]{1,0:T(8,128)S(1)}, u32[]{:S(2)}, u32[]{:S(2)}) collective-permute-start(f32[160,256]{1,0:T(8,128)S(1)} %get-tuple-element.46), channel_id=1, source_target_pairs={{0,1},{1,0},{2,3},{3,2},{4,5},{5,4},{6,7},{7,6},{8,9},{9,8},{10,11... | collective-permute-start | bytes 491528 | tf_op jit(solution)/shard_map/ppermute | solution.py:401
  136.8 4.4 %collective-permute-done.25 = f32[4,96,256]{2,1,0:T(8,128)} collective-permute-done((f32[4,96,256]{2,1,0:T(8,128)}, f32[4,96,256]{2,1,0:T(8,128)}, u32[]{:S(2)}, u32[]{:S(2)}) %collective-permute-start.25) | collective-permute-done | bytes 393248 | tf_op jit(solution)/shard_map/ppermute | solution.py:401
  141.1 1.1 fusion.3
  142.2 2.0 %collective-permute-start.26 = (f32[96,256]{1,0:T(8,128)S(1)}, f32[96,256]{1,0:T(8,128)S(1)}, u32[]{:S(2)}, u32[]{:S(2)}) collective-permute-start(f32[96,256]{1,0:T(8,128)S(1)} %get-tuple-element.44), channel_id=1, source_target_pairs={{0,2},{1,3},{2,0},{3,1},{4,6},{5,7},{6,4},{7,5},{8,10},{9,11},{10,... | collective-permute-start | bytes 294920 | tf_op jit(solution)/shard_map/ppermute | solution.py:401
  144.3 4.2 %collective-permute-start.27 = (f32[96,256]{1,0:T(8,128)S(1)}, f32[96,256]{1,0:T(8,128)S(1)}, u32[]{:S(2)}, u32[]{:S(2)}) collective-permute-start(f32[96,256]{1,0:T(8,128)S(1)} %get-tuple-element.43), channel_id=1, source_target_pairs={{0,4},{1,5},{2,6},{3,7},{4,0},{5,1},{6,2},{7,3},{8,12},{9,13},{10,... | collective-permute-start | bytes 294920 | tf_op jit(solution)/shard_map/ppermute | solution.py:401
  148.5 0.3 collective-permute-start.28
  148.8 1.4 shard_map.55.refs_4_
  150.2 0.9 collective-permute-start.34
  151.1 3.6 %collective-permute-start.35 = (f32[384,128]{1,0:T(8,128)S(1)}, f32[384,128]{1,0:T(8,128)S(1)}, u32[]{:S(2)}, u32[]{:S(2)}) collective-permute-start(f32[384,128]{1,0:T(8,128)S(1)} %shard_map.55.refs_4_), channel_id=1, source_target_pairs={{0,4},{1,5},{2,6},{3,7},{4,0},{5,1},{6,2},{7,3},{8,12},{9,13},{10,... | collective-permute-start | bytes 589832 | tf_op jit(solution)/shard_map/ppermute | solution.py:401
  154.7 0.3 collective-permute-start.36
  154.9 1.3 fusion.1.one_ref
  156.2 1.7 collective-permute-done.28.d
  157.9 0.7 shard_map.54
  158.7 1.9 %collective-permute-start.29 = (bf16[256,256]{1,0:T(8,128)(2,1)S(1)}, bf16[256,256]{1,0:T(8,128)(2,1)S(1)}, u32[]{:S(2)}, u32[]{:S(2)}) collective-permute-start(bf16[256,256]{1,0:T(8,128)(2,1)S(1)} %get-tuple-element.34), channel_id=1, source_target_pairs={{1,19},{5,131},{0,16},{2,8},{6,128},{7,35},{4,163},{3,101},{9,120}... | collective-permute-start | bytes 393224 | tf_op jit(solution)/shard_map/ppermute | solution.py:497
  160.6 6.4 %collective-permute-start.30 = (bf16[256,256]{1,0:T(8,128)(2,1)S(1)}, bf16[256,256]{1,0:T(8,128)(2,1)S(1)}, u32[]{:S(2)}, u32[]{:S(2)}) collective-permute-start(bf16[256,256]{1,0:T(8,128)(2,1)S(1)} %get-tuple-element.35), channel_id=1, source_target_pairs={{1,112},{7,120},{5,116},{2,16},{0,19},{6,131},{4,125},{3,163},{10,... | collective-permute-start | bytes 393224 | tf_op jit(solution)/shard_map/ppermute | solution.py:497
  167.0 1.6 collective-permute-start.31
  168.6 5.8 %collective-permute-start.32 = (bf16[256,256]{1,0:T(8,128)(2,1)S(1)}, bf16[256,256]{1,0:T(8,128)(2,1)S(1)}, u32[]{:S(2)}, u32[]{:S(2)}) collective-permute-start(bf16[256,256]{1,0:T(8,128)(2,1)S(1)} %get-tuple-element.37), channel_id=1, source_target_pairs={{3,131},{0,0},{6,4},{1,19},{2,108},{7,97},{5,163},{13,116},{10,104... | collective-permute-start | bytes 393224 | tf_op jit(solution)/shard_map/ppermute | solution.py:497
  174.4 0.6 collective-permute-start.37
  175.0 3.1 %collective-permute-done.32.refs_3_ = bf16[256,256]{1,0:T(8,128)(2,1)S(1)} collective-permute-done((bf16[256,256]{1,0:T(8,128)(2,1)S(1)}, bf16[256,256]{1,0:T(8,128)(2,1)S(1)}, u32[]{:S(2)}, u32[]{:S(2)}) %collective-permute-start.32) | collective-permute-done | bytes 131104 | tf_op jit(solution)/shard_map/ppermute | solution.py:497
  178.1 3.1 %collective-permute-done.37.refs_9_ = f32[256,128]{1,0:T(8,128)S(1)} collective-permute-done((f32[256,128]{1,0:T(8,128)S(1)}, f32[256,128]{1,0:T(8,128)S(1)}, u32[]{:S(2)}, u32[]{:S(2)}) %collective-permute-start.37) | collective-permute-done | bytes 131104 | tf_op jit(solution)/shard_map/ppermute | solution.py:401
  181.2 1.6 shard_map.56
  (56 shorter events, 1.1 us)
Async XLA Ops:
  0.6 4.3 %copy-start = (bf16[2048,128]{1,0:T(8,128)(2,1)S(1)}, bf16[2048,128]{1,0:T(8,128)(2,1)}, u32[]{:S(2)}) copy-start(bf16[2048,128]{1,0:T(8,128)(2,1)} %param.4) | copy-start | bytes 1572868
  0.6 4.0 %copy-start.1 = (bf16[256,2048]{1,0:T(8,128)(2,1)S(1)}, bf16[256,2048]{1,0:T(8,128)(2,1)}, u32[]{:S(2)}) copy-start(bf16[256,2048]{1,0:T(8,128)(2,1)} %own.3) | copy-start | bytes 3145732
  2.9 13.8 %collective-permute-start.3 = (bf16[128,2048]{1,0:T(8,128)(2,1)S(1)}, bf16[128,2048]{1,0:T(8,128)(2,1)S(1)}, u32[]{:S(2)}, u32[]{:S(2)}) collective-permute-start(bf16[128,2048]{1,0:T(8,128)(2,1)S(1)} %get-tuple-element.41), channel_id=1, source_target_pairs={{0,112},{8,120},{16,0},{24,8},{32,16},{40,24},{48,32},{56,40},{64,... | collective-permute-start | bytes 1572872 | tf_op jit(solution)/shard_map/ppermute | solution.py:398
  4.7 27.2 %collective-permute-start = (bf16[256,2048]{1,0:T(8,128)(2,1)S(1)}, bf16[256,2048]{1,0:T(8,128)(2,1)}, u32[]{:S(2)}, u32[]{:S(2)}) collective-permute-start(bf16[256,2048]{1,0:T(8,128)(2,1)S(1)} %copy-done.1), channel_id=1, source_target_pairs={{0,16},{8,24},{16,32},{24,40},{32,48},{40,56},{48,64},{56,72},{64,... | collective-permute-start | bytes 3145736 | tf_op jit(solution)/shard_map/ppermute | solution.py:398
  5.3 14.7 %collective-permute-start.15 = (f32[256,128]{1,0:T(8,128)S(1)}, f32[256,128]{1,0:T(8,128)S(1)}, u32[]{:S(2)}, u32[]{:S(2)}) collective-permute-start(f32[256,128]{1,0:T(8,128)S(1)} %fusion.8), channel_id=1, source_target_pairs={{0,4},{1,5},{2,6},{3,7},{4,0},{5,1},{6,2},{7,3},{8,12},{9,13},{10,... | collective-permute-start | bytes 393224 | tf_op jit(solution)/shard_map/ppermute | solution.py:401
  8.6 11.4 %collective-permute-start.16 = (f32[256,128]{1,0:T(8,128)S(1)}, f32[256,128]{1,0:T(8,128)S(1)}, u32[]{:S(2)}, u32[]{:S(2)}) collective-permute-start(f32[256,128]{1,0:T(8,128)S(1)} %fusion.8), channel_id=1, source_target_pairs={{0,6},{1,7},{2,4},{3,5},{4,2},{5,3},{6,0},{7,1},{8,14},{9,15},{10,... | collective-permute-start | bytes 393224 | tf_op jit(solution)/shard_map/ppermute | solution.py:401
  9.7 10.4 %collective-permute-start.14 = (f32[256,128]{1,0:T(8,128)S(1)}, f32[256,128]{1,0:T(8,128)S(1)}, u32[]{:S(2)}, u32[]{:S(2)}) collective-permute-start(f32[256,128]{1,0:T(8,128)S(1)} %fusion.8), channel_id=1, source_target_pairs={{0,2},{1,3},{2,0},{3,1},{4,6},{5,7},{6,4},{7,5},{8,10},{9,11},{10,... | collective-permute-start | bytes 393224 | tf_op jit(solution)/shard_map/ppermute | solution.py:401
  16.7 66.6 %copy-start.4 = (bf16[128,2048]{1,0:T(8,128)(2,1)}, bf16[128,2048]{1,0:T(8,128)(2,1)S(1)}, u32[]{:S(2)}) copy-start(bf16[128,2048]{1,0:T(8,128)(2,1)S(1)} %collective-permute-done.3.refs_4_.refs_2_) | copy-start | bytes 1572868
  16.7 13.6 %collective-permute-start.12 = (bf16[128,2048]{1,0:T(8,128)(2,1)S(1)}, bf16[128,2048]{1,0:T(8,128)(2,1)}, u32[]{:S(2)}, u32[]{:S(2)}) collective-permute-start(bf16[128,2048]{1,0:T(8,128)(2,1)S(1)} %collective-permute-done.3.refs_4_.refs_2_), channel_id=1, source_target_pairs={{0,112},{8,120},{16,0},{24,8},{32,16},{40,24},{48,32},{56,40},{64,... | collective-permute-start | bytes 1572872 | tf_op jit(solution)/shard_map/ppermute | solution.py:398
  20.1 6.6 %collective-permute-start.17 = (f32[256,128]{1,0:T(8,128)S(1)}, f32[256,128]{1,0:T(8,128)S(1)}, u32[]{:S(2)}, u32[]{:S(2)}) collective-permute-start(f32[256,128]{1,0:T(8,128)S(1)} %add_add_fusion.1.part), channel_id=1, source_target_pairs={{0,1},{1,0},{2,3},{3,2},{4,5},{5,4},{6,7},{7,6},{8,9},{9,8},{10,11... | collective-permute-start | bytes 393224 | tf_op jit(solution)/shard_map/ppermute | solution.py:401
  28.2 7.4 %collective-permute-start.18 = (f32[1024,128]{1,0:T(8,128)S(1)}, f32[1024,128]{1,0:T(8,128)S(1)}, u32[]{:S(2)}, u32[]{:S(2)}) collective-permute-start(f32[1024,128]{1,0:T(8,128)S(1)} %get-tuple-element.26), channel_id=1, source_target_pairs={{0,8},{8,0},{16,24},{24,16},{32,40},{40,32},{48,56},{56,48},{64,72... | collective-permute-start | bytes 1572872 | tf_op jit(solution)/shard_map/ppermute | solution.py:398
  30.3 15.0 %collective-permute-start.19 = (bf16[128,2048]{1,0:T(8,128)(2,1)}, bf16[128,2048]{1,0:T(8,128)(2,1)S(1)}, u32[]{:S(2)}, u32[]{:S(2)}) collective-permute-start(bf16[128,2048]{1,0:T(8,128)(2,1)} %collective-permute-done.12.refs_4_), channel_id=1, source_target_pairs={{0,128},{8,136},{16,144},{24,152},{32,160},{40,168},{48,176},{56,1... | collective-permute-start | bytes 1572872 | tf_op jit(solution)/shard_map/ppermute | solution.py:398
  31.8 25.4 %collective-permute-start.10 = (bf16[256,2048]{1,0:T(8,128)(2,1)}, bf16[256,2048]{1,0:T(8,128)(2,1)S(1)}, u32[]{:S(2)}, u32[]{:S(2)}) collective-permute-start(bf16[256,2048]{1,0:T(8,128)(2,1)} %collective-permute-done.refs_0_.refs_2_), channel_id=1, source_target_pairs={{0,16},{8,24},{16,32},{24,40},{32,48},{40,56},{48,64},{56,72},{64,... | collective-permute-start | bytes 3145736 | tf_op jit(solution)/shard_map/ppermute | solution.py:398
  34.6 22.2 %collective-permute-start.4 = (bf16[128,2048]{1,0:T(8,128)(2,1)}, bf16[128,2048]{1,0:T(8,128)(2,1)}, u32[]{:S(2)}, u32[]{:S(2)}) collective-permute-start(bf16[128,2048]{1,0:T(8,128)(2,1)} %get-tuple-element.40), channel_id=1, source_target_pairs={{0,112},{8,120},{16,0},{24,8},{32,16},{40,24},{48,32},{56,40},{64,... | collective-permute-start | bytes 1572872 | tf_op jit(solution)/shard_map/ppermute | solution.py:398
  35.5 47.8 %collective-permute-start.2 = (bf16[256,2048]{1,0:T(8,128)(2,1)S(1)}, bf16[256,2048]{1,0:T(8,128)(2,1)}, u32[]{:S(2)}, u32[]{:S(2)}) collective-permute-start(bf16[256,2048]{1,0:T(8,128)(2,1)S(1)} %copy-done.1), channel_id=1, source_target_pairs={{0,8},{8,0},{16,24},{24,16},{32,40},{40,32},{48,56},{56,48},{64,72... | collective-permute-start | bytes 3145736 | tf_op jit(solution)/shard_map/ppermute | solution.py:398
  35.5 47.8 %collective-permute-start.5 = (bf16[256,2048]{1,0:T(8,128)(2,1)S(1)}, bf16[256,2048]{1,0:T(8,128)(2,1)}, u32[]{:S(2)}, u32[]{:S(2)}) collective-permute-start(bf16[256,2048]{1,0:T(8,128)(2,1)S(1)} %copy-done.1), channel_id=1, source_target_pairs={{0,128},{8,136},{16,144},{24,152},{32,160},{40,168},{48,176},{56,1... | collective-permute-start | bytes 3145736 | tf_op jit(solution)/shard_map/ppermute | solution.py:398
  45.3 0.8 copy-start.6
  46.1 37.2 %collective-permute-start.1 = (bf16[256,2048]{1,0:T(8,128)(2,1)}, bf16[256,2048]{1,0:T(8,128)(2,1)}, u32[]{:S(2)}, u32[]{:S(2)}) collective-permute-start(bf16[256,2048]{1,0:T(8,128)(2,1)} %collective-permute-done.refs_0_.refs_2_), channel_id=1, source_target_pairs={{0,8},{8,0},{16,24},{24,16},{32,40},{40,32},{48,56},{56,48},{64,72... | collective-permute-start | bytes 3145736 | tf_op jit(solution)/shard_map/ppermute | solution.py:398
  47.1 47.6 %all-to-all-start = ((f32[16,64,128]{2,1,0:T(8,128)}), f32[16,64,128]{2,1,0:T(8,128)}, u32[]{:S(2)}, u32[]{:S(2)}) async-start(f32[16,64,128]{2,1,0:T(8,128)} %bitcast.20), calls=%async_computation | async-start | bytes 1048576 | tf_op jit(solution)/shard_map/all_to_all | solution.py:213
  56.8 25.1 %collective-permute-start.13 = (bf16[128,2048]{1,0:T(8,128)(2,1)}, bf16[128,2048]{1,0:T(8,128)(2,1)}, u32[]{:S(2)}, u32[]{:S(2)}) collective-permute-start(bf16[128,2048]{1,0:T(8,128)(2,1)} %collective-permute-done.4.refs_5_.refs_3_), channel_id=1, source_target_pairs={{0,112},{8,120},{16,0},{24,8},{32,16},{40,24},{48,32},{56,40},{64,... | collective-permute-start | bytes 1572872 | tf_op jit(solution)/shard_map/ppermute | solution.py:398
  57.2 45.6 %collective-permute-start.11 = (bf16[256,2048]{1,0:T(8,128)(2,1)S(1)}, bf16[256,2048]{1,0:T(8,128)(2,1)}, u32[]{:S(2)}, u32[]{:S(2)}) collective-permute-start(bf16[256,2048]{1,0:T(8,128)(2,1)S(1)} %collective-permute-done.10.refs_0_), channel_id=1, source_target_pairs={{0,8},{8,0},{16,24},{24,16},{32,40},{40,32},{48,56},{56,48},{64,72... | collective-permute-start | bytes 3145736 | tf_op jit(solution)/shard_map/ppermute | solution.py:398
  81.8 25.1 %collective-permute-start.20 = (bf16[128,2048]{1,0:T(8,128)(2,1)}, bf16[128,2048]{1,0:T(8,128)(2,1)}, u32[]{:S(2)}, u32[]{:S(2)}) collective-permute-start(bf16[128,2048]{1,0:T(8,128)(2,1)} %collective-permute-done.13.refs_5_), channel_id=1, source_target_pairs={{0,128},{8,136},{16,144},{24,152},{32,160},{40,168},{48,176},{56,1... | collective-permute-start | bytes 1572872 | tf_op jit(solution)/shard_map/ppermute | solution.py:398
  89.7 0.8 copy-start.2
  90.5 31.3 %collective-permute-start.8 = (f32[576,256]{1,0:T(8,128)}, f32[576,256]{1,0:T(8,128)}, u32[]{:S(2)}, u32[]{:S(2)}) collective-permute-start(f32[576,256]{1,0:T(8,128)} %get-tuple-element.24), channel_id=1, source_target_pairs={{0,6},{1,7},{2,4},{3,5},{4,2},{5,3},{6,0},{7,1},{8,14},{9,15},{10,... | collective-permute-start | bytes 1769480 | tf_op jit(solution)/shard_map/ppermute | solution.py:401
  93.6 28.9 %collective-permute-start.7 = (f32[576,256]{1,0:T(8,128)}, f32[576,256]{1,0:T(8,128)}, u32[]{:S(2)}, u32[]{:S(2)}) collective-permute-start(f32[576,256]{1,0:T(8,128)} %get-tuple-element.23), channel_id=1, source_target_pairs={{0,4},{1,5},{2,6},{3,7},{4,0},{5,1},{6,2},{7,3},{8,12},{9,13},{10,... | collective-permute-start | bytes 1769480 | tf_op jit(solution)/shard_map/ppermute | solution.py:401
  94.2 28.2 %collective-permute-start.6 = (f32[576,256]{1,0:T(8,128)}, f32[576,256]{1,0:T(8,128)}, u32[]{:S(2)}, u32[]{:S(2)}) collective-permute-start(f32[576,256]{1,0:T(8,128)} %get-tuple-element.22), channel_id=1, source_target_pairs={{0,2},{1,3},{2,0},{3,1},{4,6},{5,7},{6,4},{7,5},{8,10},{9,11},{10,... | collective-permute-start | bytes 1769480 | tf_op jit(solution)/shard_map/ppermute | solution.py:401
  96.6 37.2 %all-to-all-start.1 = ((f32[16,64,128]{2,1,0:T(8,128)}), f32[16,64,128]{2,1,0:T(8,128)S(1)}, u32[]{:S(2)}, u32[]{:S(2)}) async-start(f32[16,64,128]{2,1,0:T(8,128)} %broadcast_in_dim.3), calls=%async_computation.1 | async-start | bytes 1048576 | tf_op jit(solution)/shard_map/all_to_all | solution.py:213
  102.8 1.0 copy-start.5
  103.9 3.1 %copy-start.7 = (bf16[128,2048]{1,0:T(8,128)(2,1)S(1)}, bf16[128,2048]{1,0:T(8,128)(2,1)}, u32[]{:S(2)}) copy-start(bf16[128,2048]{1,0:T(8,128)(2,1)} %copy-done.6) | copy-start | bytes 1572868
  107.0 15.5 %copy-start.3 = (f32[576,256]{1,0:T(8,128)S(1)}, f32[576,256]{1,0:T(8,128)}, u32[]{:S(2)}) copy-start(f32[576,256]{1,0:T(8,128)} %copy-done.2) | copy-start | bytes 1769476
  111.8 11.9 %copy-start.8 = (f32[4,96,256]{2,1,0:T(8,128)}, f32[4,96,256]{2,1,0:T(8,128)S(1)}, u32[]{:S(2)}) copy-start(f32[4,96,256]{2,1,0:T(8,128)S(1)} %get-tuple-element.32) | copy-start | bytes 1179652
  111.8 19.4 %collective-permute-start.22 = (f32[2,160,256]{2,1,0:T(8,128)S(1)}, f32[2,160,256]{2,1,0:T(8,128)S(1)}, u32[]{:S(2)}, u32[]{:S(2)}) collective-permute-start(f32[2,160,256]{2,1,0:T(8,128)S(1)} %get-tuple-element.30), channel_id=1, source_target_pairs={{0,4},{1,5},{2,6},{3,7},{4,0},{5,1},{6,2},{7,3},{8,12},{9,13},{10,... | collective-permute-start | bytes 983048 | tf_op jit(solution)/shard_map/ppermute | solution.py:401
  115.0 18.1 %collective-permute-start.23 = (f32[2,160,256]{2,1,0:T(8,128)S(1)}, f32[2,160,256]{2,1,0:T(8,128)S(1)}, u32[]{:S(2)}, u32[]{:S(2)}) collective-permute-start(f32[2,160,256]{2,1,0:T(8,128)S(1)} %get-tuple-element.31), channel_id=1, source_target_pairs={{0,6},{1,7},{2,4},{3,5},{4,2},{5,3},{6,0},{7,1},{8,14},{9,15},{10,... | collective-permute-start | bytes 983048 | tf_op jit(solution)/shard_map/ppermute | solution.py:401
  121.8 11.9 %collective-permute-start.21 = (f32[2,160,256]{2,1,0:T(8,128)S(1)}, f32[2,160,256]{2,1,0:T(8,128)S(1)}, u32[]{:S(2)}, u32[]{:S(2)}) collective-permute-start(f32[2,160,256]{2,1,0:T(8,128)S(1)} %get-tuple-element.29), channel_id=1, source_target_pairs={{0,2},{1,3},{2,0},{3,1},{4,6},{5,7},{6,4},{7,5},{8,10},{9,11},{10,... | collective-permute-start | bytes 983048 | tf_op jit(solution)/shard_map/ppermute | solution.py:401
  123.7 24.8 %collective-permute-start.9 = (f32[320,256]{1,0:T(8,128)S(1)}, f32[320,256]{1,0:T(8,128)S(1)}, u32[]{:S(2)}, u32[]{:S(2)}) collective-permute-start(f32[320,256]{1,0:T(8,128)S(1)} %fusion.one), channel_id=1, source_target_pairs={{0,1},{1,0},{2,3},{3,2},{4,5},{5,4},{6,7},{7,6},{8,9},{9,8},{10,11... | collective-permute-start | bytes 983048 | tf_op jit(solution)/shard_map/ppermute | solution.py:401
  126.5 14.6 %collective-permute-start.25 = (f32[4,96,256]{2,1,0:T(8,128)}, f32[4,96,256]{2,1,0:T(8,128)}, u32[]{:S(2)}, u32[]{:S(2)}) collective-permute-start(f32[4,96,256]{2,1,0:T(8,128)} %get-tuple-element.33), channel_id=1, source_target_pairs={{0,1},{1,0},{2,3},{3,2},{4,5},{5,4},{6,7},{7,6},{8,9},{9,8},{10,11... | collective-permute-start | bytes 1179656 | tf_op jit(solution)/shard_map/ppermute | solution.py:401
  133.8 7.3 %copy-start.9 = (f32[4,96,256]{2,1,0:T(8,128)S(1)}, f32[4,96,256]{2,1,0:T(8,128)}, u32[]{:S(2)}) copy-start(f32[4,96,256]{2,1,0:T(8,128)} %copy-done.8) | copy-start | bytes 1179652
  133.8 15.0 %collective-permute-start.33 = (f32[1024,128]{1,0:T(8,128)S(1)}, f32[1024,128]{1,0:T(8,128)S(1)}, u32[]{:S(2)}, u32[]{:S(2)}) collective-permute-start(f32[1024,128]{1,0:T(8,128)S(1)} %bitcast.18), channel_id=1, source_target_pairs={{0,8},{8,0},{16,24},{24,16},{32,40},{40,32},{48,56},{56,48},{64,72... | collective-permute-start | bytes 1572872 | tf_op jit(solution)/shard_map/ppermute | solution.py:398
  133.9 17.2 %collective-permute-start.24 = (f32[160,256]{1,0:T(8,128)S(1)}, f32[160,256]{1,0:T(8,128)S(1)}, u32[]{:S(2)}, u32[]{:S(2)}) collective-permute-start(f32[160,256]{1,0:T(8,128)S(1)} %get-tuple-element.46), channel_id=1, source_target_pairs={{0,1},{1,0},{2,3},{3,2},{4,5},{5,4},{6,7},{7,6},{8,9},{9,8},{10,11... | collective-permute-start | bytes 491528 | tf_op jit(solution)/shard_map/ppermute | solution.py:401
  142.2 12.4 %collective-permute-start.26 = (f32[96,256]{1,0:T(8,128)S(1)}, f32[96,256]{1,0:T(8,128)S(1)}, u32[]{:S(2)}, u32[]{:S(2)}) collective-permute-start(f32[96,256]{1,0:T(8,128)S(1)} %get-tuple-element.44), channel_id=1, source_target_pairs={{0,2},{1,3},{2,0},{3,1},{4,6},{5,7},{6,4},{7,5},{8,10},{9,11},{10,... | collective-permute-start | bytes 294920 | tf_op jit(solution)/shard_map/ppermute | solution.py:401
  144.3 11.9 %collective-permute-start.27 = (f32[96,256]{1,0:T(8,128)S(1)}, f32[96,256]{1,0:T(8,128)S(1)}, u32[]{:S(2)}, u32[]{:S(2)}) collective-permute-start(f32[96,256]{1,0:T(8,128)S(1)} %get-tuple-element.43), channel_id=1, source_target_pairs={{0,4},{1,5},{2,6},{3,7},{4,0},{5,1},{6,2},{7,3},{8,12},{9,13},{10,... | collective-permute-start | bytes 294920 | tf_op jit(solution)/shard_map/ppermute | solution.py:401
  148.5 9.4 %collective-permute-start.28 = (f32[96,256]{1,0:T(8,128)S(1)}, f32[96,256]{1,0:T(8,128)S(1)}, u32[]{:S(2)}, u32[]{:S(2)}) collective-permute-start(f32[96,256]{1,0:T(8,128)S(1)} %get-tuple-element.42), channel_id=1, source_target_pairs={{0,6},{1,7},{2,4},{3,5},{4,2},{5,3},{6,0},{7,1},{8,14},{9,15},{10,... | collective-permute-start | bytes 294920 | tf_op jit(solution)/shard_map/ppermute | solution.py:401
  150.2 16.8 %collective-permute-start.34 = (f32[384,128]{1,0:T(8,128)S(1)}, f32[384,128]{1,0:T(8,128)S(1)}, u32[]{:S(2)}, u32[]{:S(2)}) collective-permute-start(f32[384,128]{1,0:T(8,128)S(1)} %shard_map.55.refs_4_), channel_id=1, source_target_pairs={{0,2},{1,3},{2,0},{3,1},{4,6},{5,7},{6,4},{7,5},{8,10},{9,11},{10,... | collective-permute-start | bytes 589832 | tf_op jit(solution)/shard_map/ppermute | solution.py:401
  151.1 17.5 %collective-permute-start.35 = (f32[384,128]{1,0:T(8,128)S(1)}, f32[384,128]{1,0:T(8,128)S(1)}, u32[]{:S(2)}, u32[]{:S(2)}) collective-permute-start(f32[384,128]{1,0:T(8,128)S(1)} %shard_map.55.refs_4_), channel_id=1, source_target_pairs={{0,4},{1,5},{2,6},{3,7},{4,0},{5,1},{6,2},{7,3},{8,12},{9,13},{10,... | collective-permute-start | bytes 589832 | tf_op jit(solution)/shard_map/ppermute | solution.py:401
  154.7 19.7 %collective-permute-start.36 = (f32[384,128]{1,0:T(8,128)S(1)}, f32[384,128]{1,0:T(8,128)S(1)}, u32[]{:S(2)}, u32[]{:S(2)}) collective-permute-start(f32[384,128]{1,0:T(8,128)S(1)} %shard_map.55.refs_4_), channel_id=1, source_target_pairs={{0,6},{1,7},{2,4},{3,5},{4,2},{5,3},{6,0},{7,1},{8,14},{9,15},{10,... | collective-permute-start | bytes 589832 | tf_op jit(solution)/shard_map/ppermute | solution.py:401
  158.7 16.3 %collective-permute-start.29 = (bf16[256,256]{1,0:T(8,128)(2,1)S(1)}, bf16[256,256]{1,0:T(8,128)(2,1)S(1)}, u32[]{:S(2)}, u32[]{:S(2)}) collective-permute-start(bf16[256,256]{1,0:T(8,128)(2,1)S(1)} %get-tuple-element.34), channel_id=1, source_target_pairs={{1,19},{5,131},{0,16},{2,8},{6,128},{7,35},{4,163},{3,101},{9,120}... | collective-permute-start | bytes 393224 | tf_op jit(solution)/shard_map/ppermute | solution.py:497
  160.6 14.4 %collective-permute-start.30 = (bf16[256,256]{1,0:T(8,128)(2,1)S(1)}, bf16[256,256]{1,0:T(8,128)(2,1)S(1)}, u32[]{:S(2)}, u32[]{:S(2)}) collective-permute-start(bf16[256,256]{1,0:T(8,128)(2,1)S(1)} %get-tuple-element.35), channel_id=1, source_target_pairs={{1,112},{7,120},{5,116},{2,16},{0,19},{6,131},{4,125},{3,163},{10,... | collective-permute-start | bytes 393224 | tf_op jit(solution)/shard_map/ppermute | solution.py:497
  167.0 8.0 %collective-permute-start.31 = (bf16[256,256]{1,0:T(8,128)(2,1)S(1)}, bf16[256,256]{1,0:T(8,128)(2,1)S(1)}, u32[]{:S(2)}, u32[]{:S(2)}) collective-permute-start(bf16[256,256]{1,0:T(8,128)(2,1)S(1)} %get-tuple-element.36), channel_id=1, source_target_pairs={{7,19},{3,124},{4,8},{1,96},{0,104},{6,100},{2,131},{5,117},{9,27}... | collective-permute-start | bytes 393224 | tf_op jit(solution)/shard_map/ppermute | solution.py:497
  168.6 9.5 %collective-permute-start.32 = (bf16[256,256]{1,0:T(8,128)(2,1)S(1)}, bf16[256,256]{1,0:T(8,128)(2,1)S(1)}, u32[]{:S(2)}, u32[]{:S(2)}) collective-permute-start(bf16[256,256]{1,0:T(8,128)(2,1)S(1)} %get-tuple-element.37), channel_id=1, source_target_pairs={{3,131},{0,0},{6,4},{1,19},{2,108},{7,97},{5,163},{13,116},{10,104... | collective-permute-start | bytes 393224 | tf_op jit(solution)/shard_map/ppermute | solution.py:497
  174.4 6.7 %collective-permute-start.37 = (f32[256,128]{1,0:T(8,128)S(1)}, f32[256,128]{1,0:T(8,128)S(1)}, u32[]{:S(2)}, u32[]{:S(2)}) collective-permute-start(f32[256,128]{1,0:T(8,128)S(1)} %fusion.2.refs_8_), channel_id=1, source_target_pairs={{0,1},{1,0},{2,3},{3,2},{4,5},{5,4},{6,7},{7,6},{8,9},{9,8},{10,11... | collective-permute-start | bytes 393224 | tf_op jit(solution)/shard_map/ppermute | solution.py:401

commit v2 on v1

--- a/solution.py
+++ b/solution.py
@@ -98,6 +98,10 @@
     return f % 2 * 2 + i // (2 * NZ), f // 2, i // 2 % NZ
 
 
+def hops(src, dst):
+    return sum(min((x - y) % n, (y - x) % n) for x, y, n in zip(src, dst, SIZES))
+
+
 def links(src, dst, memo):
     if (src, dst) not in memo:
         at, part = [], []
@@ -130,11 +134,7 @@
                 ends = [chip(r, c // per), chip(c, r // per)][: 1 if (round_, slot) == (0, 6) else 2]
                 owners[i, round_, slot] = ends
                 for f in range(NF):
-                    hops = [
-                        sum(min((x - y) % n, (y - x) % n) for x, y, n in zip(chip(i, f), dst, SIZES))
-                        for dst in ends
-                    ]
-                    far[i, round_, slot, f] = 30 * sum(h**3 for h in hops)
+                    far[i, round_, slot, f] = 30 * sum(hops(chip(i, f), dst) ** 3 for dst in ends)
 
     def put(key, f, weight):
         for dst in owners[key]:
@@ -177,6 +177,8 @@
                 if not (round_ == 0 and slot == 6):
                     edges.append((src, c * NF + r // per))
                     what.append((2 * round_ + 1, r % per))
+    by_hops = sorted(range(len(edges)), key=lambda e: -hops(*(chip(*divmod(x, NF)) for x in edges[e])))
+    edges, what = [edges[e] for e in by_hops], [what[e] for e in by_hops]
     colour = colour_edges(edges, 4)
     n = len(PLACES) * NF
     perms = [[] for _ in range(4)]
@@ -250,6 +252,14 @@
         @pl.when(info[CORE] != at)
         def _():
             other[...] = rows
+
+
+def share_kernel(info, parts, out):
+    total = parts[0]
+    for i in range(1, parts.shape[0]):
+        total = total + parts[i]
+    for i in range(parts.shape[0]):
+        out[i] = total
 
 
 def gdot_kernel(info, own, mine, other, first, one, one_, out):
@@ -449,8 +459,8 @@
     mine, far[0] = lax.optimization_barrier((mine, far[0]))
     chips = 2 * NZ
     mine = exchange(mine.reshape(chips, -1, mine.shape[1]), "dp", CHIP_GROUPS)
-    mine = mine.sum(axis=0)
-    mine = exchange(jnp.broadcast_to(mine, (chips, *mine.shape)), "dp", CHIP_GROUPS)
+    (mine,) = call(share_kernel, info, (mine,), [array(f32, *mine.shape)])
+    mine = exchange(mine, "dp", CHIP_GROUPS)
     mine = mine.reshape(half, -1)
 
     down2_ = move(down2, OTHER_CORE)

time: 186 us -> 188 us (1.011)
  waiting for transfers between devices: 70.3 us -> 68 us
  local copies, waits for them, and re-layouts: 6.44 us -> 8.46 us
    ppermute x20, waiting for transfers between devices: 24.1 us -> 20 us  [from_feat(): return lax.ppermute(x, 'feat', [(f, f ^ s) for f in range(NF)])]
    unnamed x20 -> x24, local copies, waits for them, and re-layouts: 2.68 us -> 4.5 us
    pallas_call x7 -> x8, Pallas kernels: 19.4 us -> 20.1 us  [call(): pl.pallas_call(kernel, in_specs=[pl.BlockSpec(memory_space=pltpu.SMEM)] +...]
where the time goes in v2:
time: 188 us; the launch traced here: 184 us
  starting transfers between devices  80.7 us (43%)
  waiting for transfers between devices  68 us (36%)
  Pallas kernels  20.1 us (11%)
  local copies, waits for them, and re-layouts  8.46 us (5%)
  other arithmetic  5.4 us (3%)
    ppermute x14, waiting for transfers between devices, move(): return lax.ppermute(x, 'dp', perm)  43.1 us
    ppermute x20, starting transfers between devices, from_feat(): return lax.ppermute(x, 'feat', [(f, f ^ s) for f in range(NF)])  35.8 us
    pallas_call x8, Pallas kernels, call(): pl.pallas_call(kernel, in_specs=[pl.BlockSpec(memory_space=pltpu.SMEM)] +...  20.1 us
    ppermute x20, waiting for transfers between devices, from_feat(): return lax.ppermute(x, 'feat', [(f, f ^ s) for f in range(NF)])  20 us
    all_to_all x2, starting transfers between devices, exchange(): lax.all_to_all(value, axis, split_axis=0, concat_axis=0, tiled=True, axis...  16 us
    ppermute x4, starting transfers between devices, body(): got.append(lax.ppermute(out[c], ('dp', 'feat'), perms[c]))  16 us
    ppermute x14, starting transfers between devices, move(): return lax.ppermute(x, 'dp', perm)  13 us
    ppermute x4, waiting for transfers between devices, body(): got.append(lax.ppermute(out[c], ('dp', 'feat'), perms[c]))  4.87 us
  transfers between devices with their start and end apart: 40, of which 14 were waited for; matrix products, arithmetic and copies ran while one was open for 4% of the time, Pallas kernels for 10%

profile of v2, /device:TPU:32, one launch (start us, length us, event | category | flops | bytes accessed | tf_op | source)
XLA Modules:
  0.0 184.0 jit_solution(1612213060637883013)
XLA Ops:
  0.7 2.2 %fusion.7 = (bf16[128,2048]{1,0:T(8,128)(2,1)}, bf16[128,2048]{1,0:T(8,128)(2,1)S(1)}) fusion(bf16[256,2048]{1,0:T(8,128)(2,1)} %own.3), kind=kLoop, calls=%fused_computation.22 | loop fusion | bytes 2097152 | tf_op jit(solution)/shard_map/slice | solution.py:420
  2.9 1.8 collective-permute-start.3
  5.3 3.3 %collective-permute-start.15 = (f32[256,128]{1,0:T(8,128)S(1)}, f32[256,128]{1,0:T(8,128)S(1)}, u32[]{:S(2)}, u32[]{:S(2)}) collective-permute-start(f32[256,128]{1,0:T(8,128)S(1)} %fusion.8), channel_id=1, source_target_pairs={{0,4},{1,5},{2,6},{3,7},{4,0},{5,1},{6,2},{7,3},{8,12},{9,13},{10,... | collective-permute-start | bytes 393224 | tf_op jit(solution)/shard_map/ppermute | solution.py:411
  8.6 1.1 collective-permute-start.16
  9.7 7.0 %collective-permute-done.3.refs_4_.refs_2_ = bf16[128,2048]{1,0:T(8,128)(2,1)S(1)} collective-permute-done((bf16[128,2048]{1,0:T(8,128)(2,1)S(1)}, bf16[128,2048]{1,0:T(8,128)(2,1)S(1)}, u32[]{:S(2)}, u32[]{:S(2)}) %collective-permute-start.3) | collective-permute-done | bytes 524320 | tf_op jit(solution)/shard_map/ppermute | solution.py:408
  16.7 3.3 %collective-permute-start.12 = (bf16[128,2048]{1,0:T(8,128)(2,1)S(1)}, bf16[128,2048]{1,0:T(8,128)(2,1)}, u32[]{:S(2)}, u32[]{:S(2)}) collective-permute-start(bf16[128,2048]{1,0:T(8,128)(2,1)S(1)} %collective-permute-done.3.refs_4_.refs_2_), channel_id=1, source_target_pairs={{0,112},{8,120},{16,0},{24,8},{32,16},{40,24},{48,32},{56,40},{64,... | collective-permute-start | bytes 1572872 | tf_op jit(solution)/shard_map/ppermute | solution.py:408
  20.1 3.1 %collective-permute-start.17 = (f32[256,128]{1,0:T(8,128)S(1)}, f32[256,128]{1,0:T(8,128)S(1)}, u32[]{:S(2)}, u32[]{:S(2)}) collective-permute-start(f32[256,128]{1,0:T(8,128)S(1)} %add_add_fusion.1.part), channel_id=1, source_target_pairs={{0,1},{1,0},{2,3},{3,2},{4,5},{5,4},{6,7},{7,6},{8,9},{9,8},{10,11... | collective-permute-start | bytes 393224 | tf_op jit(solution)/shard_map/ppermute | solution.py:411
  23.2 0.7 dynamic-slice_bitcast_fusion.info
  23.9 2.8 %collective-permute-done.17.part_ = f32[256,128]{1,0:T(8,128)S(1)} collective-permute-done((f32[256,128]{1,0:T(8,128)S(1)}, f32[256,128]{1,0:T(8,128)S(1)}, u32[]{:S(2)}, u32[]{:S(2)}) %collective-permute-start.17) | collective-permute-done | bytes 131104 | tf_op jit(solution)/shard_map/ppermute | solution.py:411
  26.6 1.5 shard_map.51
  28.3 2.1 %collective-permute-done.12.refs_4_ = bf16[128,2048]{1,0:T(8,128)(2,1)} collective-permute-done((bf16[128,2048]{1,0:T(8,128)(2,1)S(1)}, bf16[128,2048]{1,0:T(8,128)(2,1)}, u32[]{:S(2)}, u32[]{:S(2)}) %collective-permute-start.12) | collective-permute-done | bytes 524320 | tf_op jit(solution)/shard_map/ppermute | solution.py:408
  30.3 1.5 collective-permute-start.19
  31.8 2.7 %collective-permute-start.10 = (bf16[256,2048]{1,0:T(8,128)(2,1)}, bf16[256,2048]{1,0:T(8,128)(2,1)S(1)}, u32[]{:S(2)}, u32[]{:S(2)}) collective-permute-start(bf16[256,2048]{1,0:T(8,128)(2,1)} %collective-permute-done.refs_0_.refs_2_), channel_id=1, source_target_pairs={{0,16},{8,24},{16,32},{24,40},{32,48},{40,56},{48,64},{56,72},{64,... | collective-permute-start | bytes 3145736 | tf_op jit(solution)/shard_map/ppermute | solution.py:408
  34.6 0.9 collective-permute-start.4
  35.5 0.7 collective-permute-start.5
  36.3 9.1 %collective-permute-done.19.refs_6_ = bf16[128,2048]{1,0:T(8,128)(2,1)S(1)} collective-permute-done((bf16[128,2048]{1,0:T(8,128)(2,1)}, bf16[128,2048]{1,0:T(8,128)(2,1)S(1)}, u32[]{:S(2)}, u32[]{:S(2)}) %collective-permute-start.19) | collective-permute-done | bytes 524320 | tf_op jit(solution)/shard_map/ppermute | solution.py:408
  45.3 0.8 copy-done.8
  46.1 0.9 add.88
  47.0 9.7 %all-to-all-start = ((f32[16,64,128]{2,1,0:T(8,128)}), f32[16,64,128]{2,1,0:T(8,128)S(1)}, u32[]{:S(2)}, u32[]{:S(2)}) async-start(f32[16,64,128]{2,1,0:T(8,128)} %bitcast.20), calls=%async_computation | async-start | bytes 1048576 | tf_op jit(solution)/shard_map/all_to_all | solution.py:215
  57.2 24.6 %collective-permute-done.13.refs_5_ = bf16[128,2048]{1,0:T(8,128)(2,1)} collective-permute-done((bf16[128,2048]{1,0:T(8,128)(2,1)}, bf16[128,2048]{1,0:T(8,128)(2,1)}, u32[]{:S(2)}, u32[]{:S(2)}) %collective-permute-start.13) | collective-permute-done | bytes 524320 | tf_op jit(solution)/shard_map/ppermute | solution.py:408
  81.8 1.5 collective-permute-start.20
  83.3 1.0 copy-done.6
  84.3 6.4 %shard_map.50 = (f32[576,256]{1,0:T(8,128)S(1)}, f32[576,256]{1,0:T(8,128)}, f32[576,256]{1,0:T(8,128)}, f32[576,256]{1,0:T(8,128)}) custom-call(s32[28]{0:T(128)S(1)} %dynamic-slice_bitcast_fusion.info, bf16[256,2048]{1,0:T(8,128)(2,1)} %collective-permute-done.refs_0_.refs_2_, bf16[256,2048]{1,0:T(8,128)(2,1)} %collective-permute-done.1.refs_1_.refs_3_, ...), custom_call_target="tpu_custom_call" | custom-call | flops 2415919104 | bytes 8650752 | tf_op jit(solution)/shard_map/pallas_call | solution.py:382
  90.7 0.8 copy-done.3
  91.6 3.0 %collective-permute-start.8 = (f32[576,256]{1,0:T(8,128)}, f32[576,256]{1,0:T(8,128)}, u32[]{:S(2)}, u32[]{:S(2)}) collective-permute-start(f32[576,256]{1,0:T(8,128)} %get-tuple-element.24), channel_id=1, source_target_pairs={{0,6},{1,7},{2,4},{3,5},{4,2},{5,3},{6,0},{7,1},{8,14},{9,15},{10,... | collective-permute-start | bytes 1769480 | tf_op jit(solution)/shard_map/ppermute | solution.py:411
  94.6 0.6 collective-permute-start.7
  95.7 0.6 shard_map.55
  96.3 0.8 copy-done.2
  97.1 6.3 %all-to-all-start.1 = ((f32[16,64,128]{2,1,0:T(8,128)}), f32[16,64,128]{2,1,0:T(8,128)S(1)}, u32[]{:S(2)}, u32[]{:S(2)}) async-start(f32[16,64,128]{2,1,0:T(8,128)} %copy-done.2), calls=%async_computation.1 | async-start | bytes 1048576 | tf_op jit(solution)/shard_map/all_to_all | solution.py:215
  103.3 1.0 copy-done.7
  104.4 3.1 %shard_map.52.refs_8_ = f32[4,256,256]{2,1,0:T(8,128)S(1)} custom-call(s32[28]{0:T(128)S(1)} %dynamic-slice_bitcast_fusion.info, bf16[256,2048]{1,0:T(8,128)(2,1)S(1)} %collective-permute-done.10.refs_0_, bf16[256,2048]{1,0:T(8,128)(2,1)} %collective-permute-done.11.refs_1_, bf16[128,2048]{1,0:T(8,128)(2,1)S(1)} %copy-done.7, ...), custom_call_target="tpu_custom_call" | custom-call | flops 1073741824 | bytes 5242880 | tf_op jit(solution)/shard_map/pallas_call | solution.py:382
  107.5 4.8 %shard_map.53 = (f32[2,160,256]{2,1,0:T(8,128)S(1)}, f32[2,160,256]{2,1,0:T(8,128)S(1)}, f32[2,160,256]{2,1,0:T(8,128)S(1)}, f32[2,160,256]{2,1,0:T(8,128)S(1)},...) custom-call(s32[28]{0:T(128)S(1)} %dynamic-slice_bitcast_fusion.info, ...), custom_call_target="tpu_custom_call" | custom-call | flops 1073741824 | bytes 9437184 | tf_op jit(solution)/shard_map/pallas_call | solution.py:382
  112.3 3.2 %collective-permute-start.22 = (f32[2,160,256]{2,1,0:T(8,128)S(1)}, f32[2,160,256]{2,1,0:T(8,128)S(1)}, u32[]{:S(2)}, u32[]{:S(2)}) collective-permute-start(f32[2,160,256]{2,1,0:T(8,128)S(1)} %get-tuple-element.30), channel_id=1, source_target_pairs={{0,4},{1,5},{2,6},{3,7},{4,0},{5,1},{6,2},{7,3},{8,12},{9,13},{10,... | collective-permute-start | bytes 983048 | tf_op jit(solution)/shard_map/ppermute | solution.py:411
  115.5 1.1 collective-permute-start.23
  116.5 6.3 %collective-permute-done.8 = f32[576,256]{1,0:T(8,128)} collective-permute-done((f32[576,256]{1,0:T(8,128)}, f32[576,256]{1,0:T(8,128)}, u32[]{:S(2)}, u32[]{:S(2)}) %collective-permute-start.8) | collective-permute-done | bytes 589856 | tf_op jit(solution)/shard_map/ppermute | solution.py:411
  122.8 0.6 collective-permute-start.21
  123.4 1.3 fusion.one
  124.7 2.8 %collective-permute-start.9 = (f32[320,256]{1,0:T(8,128)S(1)}, f32[320,256]{1,0:T(8,128)S(1)}, u32[]{:S(2)}, u32[]{:S(2)}) collective-permute-start(f32[320,256]{1,0:T(8,128)S(1)} %fusion.one), channel_id=1, source_target_pairs={{0,1},{1,0},{2,3},{3,2},{4,5},{5,4},{6,7},{7,6},{8,9},{9,8},{10,11... | collective-permute-start | bytes 983048 | tf_op jit(solution)/shard_map/ppermute | solution.py:411
  127.5 0.8 collective-permute-start.25
  128.3 3.8 %collective-permute-done.22 = f32[2,160,256]{2,1,0:T(8,128)S(1)} collective-permute-done((f32[2,160,256]{2,1,0:T(8,128)S(1)}, f32[2,160,256]{2,1,0:T(8,128)S(1)}, u32[]{:S(2)}, u32[]{:S(2)}) %collective-permute-start.22) | collective-permute-done | bytes 327712 | tf_op jit(solution)/shard_map/ppermute | solution.py:411
  132.2 1.9 %collective-permute-done.23 = f32[2,160,256]{2,1,0:T(8,128)S(1)} collective-permute-done((f32[2,160,256]{2,1,0:T(8,128)S(1)}, f32[2,160,256]{2,1,0:T(8,128)S(1)}, u32[]{:S(2)}, u32[]{:S(2)}) %collective-permute-start.23) | collective-permute-done | bytes 327712 | tf_op jit(solution)/shard_map/ppermute | solution.py:411
  134.0 0.7 collective-permute-done.21
  134.7 0.8 add_add_fusion
  135.5 1.1 slice_bitcast_fusion
  136.6 2.8 %collective-permute-start.24 = (f32[160,256]{1,0:T(8,128)S(1)}, f32[160,256]{1,0:T(8,128)S(1)}, u32[]{:S(2)}, u32[]{:S(2)}) collective-permute-start(f32[160,256]{1,0:T(8,128)S(1)} %get-tuple-element.46), channel_id=1, source_target_pairs={{0,1},{1,0},{2,3},{3,2},{4,5},{5,4},{6,7},{7,6},{8,9},{9,8},{10,11... | collective-permute-start | bytes 491528 | tf_op jit(solution)/shard_map/ppermute | solution.py:411
  139.4 1.5 collective-permute-done.25
  140.9 1.1 fusion.3
  142.0 1.8 collective-permute-start.26
  143.9 5.5 %collective-permute-start.27 = (f32[96,256]{1,0:T(8,128)S(1)}, f32[96,256]{1,0:T(8,128)S(1)}, u32[]{:S(2)}, u32[]{:S(2)}) collective-permute-start(f32[96,256]{1,0:T(8,128)S(1)} %get-tuple-element.43), channel_id=1, source_target_pairs={{0,4},{1,5},{2,6},{3,7},{4,0},{5,1},{6,2},{7,3},{8,12},{9,13},{10,... | collective-permute-start | bytes 294920 | tf_op jit(solution)/shard_map/ppermute | solution.py:411
  149.4 0.5 collective-permute-start.28
  149.8 1.4 shard_map.56.refs_4_
  151.2 0.9 collective-permute-start.34
  152.1 3.4 %collective-permute-start.35 = (f32[384,128]{1,0:T(8,128)S(1)}, f32[384,128]{1,0:T(8,128)S(1)}, u32[]{:S(2)}, u32[]{:S(2)}) collective-permute-start(f32[384,128]{1,0:T(8,128)S(1)} %shard_map.56.refs_4_), channel_id=1, source_target_pairs={{0,4},{1,5},{2,6},{3,7},{4,0},{5,1},{6,2},{7,3},{8,12},{9,13},{10,... | collective-permute-start | bytes 589832 | tf_op jit(solution)/shard_map/ppermute | solution.py:411
  155.5 0.5 collective-permute-start.36
  156.0 1.3 fusion.1.one_ref
  157.2 1.3 collective-permute-done.28.d
  158.6 0.7 shard_map.54
  159.3 1.9 %collective-permute-start.29 = (bf16[256,256]{1,0:T(8,128)(2,1)S(1)}, bf16[256,256]{1,0:T(8,128)(2,1)S(1)}, u32[]{:S(2)}, u32[]{:S(2)}) collective-permute-start(bf16[256,256]{1,0:T(8,128)(2,1)S(1)} %get-tuple-element.34), channel_id=1, source_target_pairs={{139,228},{168,76},{201,109},{234,14},{7,35},{5,163},{8,27},{23,12... | collective-permute-start | bytes 393224 | tf_op jit(solution)/shard_map/ppermute | solution.py:507
  161.2 8.9 %collective-permute-start.30 = (bf16[256,256]{1,0:T(8,128)(2,1)S(1)}, bf16[256,256]{1,0:T(8,128)(2,1)S(1)}, u32[]{:S(2)}, u32[]{:S(2)}) collective-permute-start(bf16[256,256]{1,0:T(8,128)(2,1)S(1)} %get-tuple-element.35), channel_id=1, source_target_pairs={{3,124},{1,96},{4,163},{13,171},{18,1},{16,35},{23,176},{21,179},{... | collective-permute-start | bytes 393224 | tf_op jit(solution)/shard_map/ppermute | solution.py:507
  170.1 1.9 %collective-permute-start.31 = (bf16[256,256]{1,0:T(8,128)(2,1)S(1)}, bf16[256,256]{1,0:T(8,128)(2,1)S(1)}, u32[]{:S(2)}, u32[]{:S(2)}) collective-permute-start(bf16[256,256]{1,0:T(8,128)(2,1)S(1)} %get-tuple-element.36), channel_id=1, source_target_pairs={{37,192},{44,200},{77,233},{144,52},{193,170},{7,120},{0,19},{31,1... | collective-permute-start | bytes 393224 | tf_op jit(solution)/shard_map/ppermute | solution.py:507
  172.1 3.2 %collective-permute-start.32 = (bf16[256,256]{1,0:T(8,128)(2,1)S(1)}, bf16[256,256]{1,0:T(8,128)(2,1)S(1)}, u32[]{:S(2)}, u32[]{:S(2)}) collective-permute-start(bf16[256,256]{1,0:T(8,128)(2,1)S(1)} %get-tuple-element.37), channel_id=1, source_target_pairs={{15,171},{20,176},{103,130},{110,138},{24,43},{34,17},{32,1},{38,1... | collective-permute-start | bytes 393224 | tf_op jit(solution)/shard_map/ppermute | solution.py:507
  175.8 4.9 %collective-permute-done.31.refs_2_ = bf16[256,256]{1,0:T(8,128)(2,1)S(1)} collective-permute-done((bf16[256,256]{1,0:T(8,128)(2,1)S(1)}, bf16[256,256]{1,0:T(8,128)(2,1)S(1)}, u32[]{:S(2)}, u32[]{:S(2)}) %collective-permute-start.31) | collective-permute-done | bytes 131104 | tf_op jit(solution)/shard_map/ppermute | solution.py:507
  180.6 1.7 collective-permute-done.37.refs_9_
  182.4 1.6 shard_map.57
  (59 shorter events, 2.3 us)
Async XLA Ops:
  0.6 4.3 %copy-start = (bf16[2048,128]{1,0:T(8,128)(2,1)S(1)}, bf16[2048,128]{1,0:T(8,128)(2,1)}, u32[]{:S(2)}) copy-start(bf16[2048,128]{1,0:T(8,128)(2,1)} %param.4) | copy-start | bytes 1572868
  0.6 4.0 %copy-start.1 = (bf16[256,2048]{1,0:T(8,128)(2,1)S(1)}, bf16[256,2048]{1,0:T(8,128)(2,1)}, u32[]{:S(2)}) copy-start(bf16[256,2048]{1,0:T(8,128)(2,1)} %own.3) | copy-start | bytes 3145732
  2.9 13.8 %collective-permute-start.3 = (bf16[128,2048]{1,0:T(8,128)(2,1)S(1)}, bf16[128,2048]{1,0:T(8,128)(2,1)S(1)}, u32[]{:S(2)}, u32[]{:S(2)}) collective-permute-start(bf16[128,2048]{1,0:T(8,128)(2,1)S(1)} %get-tuple-element.41), channel_id=1, source_target_pairs={{0,112},{8,120},{16,0},{24,8},{32,16},{40,24},{48,32},{56,40},{64,... | collective-permute-start | bytes 1572872 | tf_op jit(solution)/shard_map/ppermute | solution.py:408
  4.7 27.2 %collective-permute-start = (bf16[256,2048]{1,0:T(8,128)(2,1)S(1)}, bf16[256,2048]{1,0:T(8,128)(2,1)}, u32[]{:S(2)}, u32[]{:S(2)}) collective-permute-start(bf16[256,2048]{1,0:T(8,128)(2,1)S(1)} %copy-done.1), channel_id=1, source_target_pairs={{0,16},{8,24},{16,32},{24,40},{32,48},{40,56},{48,64},{56,72},{64,... | collective-permute-start | bytes 3145736 | tf_op jit(solution)/shard_map/ppermute | solution.py:408
  5.3 14.7 %collective-permute-start.15 = (f32[256,128]{1,0:T(8,128)S(1)}, f32[256,128]{1,0:T(8,128)S(1)}, u32[]{:S(2)}, u32[]{:S(2)}) collective-permute-start(f32[256,128]{1,0:T(8,128)S(1)} %fusion.8), channel_id=1, source_target_pairs={{0,4},{1,5},{2,6},{3,7},{4,0},{5,1},{6,2},{7,3},{8,12},{9,13},{10,... | collective-permute-start | bytes 393224 | tf_op jit(solution)/shard_map/ppermute | solution.py:411
  8.6 11.4 %collective-permute-start.16 = (f32[256,128]{1,0:T(8,128)S(1)}, f32[256,128]{1,0:T(8,128)S(1)}, u32[]{:S(2)}, u32[]{:S(2)}) collective-permute-start(f32[256,128]{1,0:T(8,128)S(1)} %fusion.8), channel_id=1, source_target_pairs={{0,6},{1,7},{2,4},{3,5},{4,2},{5,3},{6,0},{7,1},{8,14},{9,15},{10,... | collective-permute-start | bytes 393224 | tf_op jit(solution)/shard_map/ppermute | solution.py:411
  9.7 10.4 %collective-permute-start.14 = (f32[256,128]{1,0:T(8,128)S(1)}, f32[256,128]{1,0:T(8,128)S(1)}, u32[]{:S(2)}, u32[]{:S(2)}) collective-permute-start(f32[256,128]{1,0:T(8,128)S(1)} %fusion.8), channel_id=1, source_target_pairs={{0,2},{1,3},{2,0},{3,1},{4,6},{5,7},{6,4},{7,5},{8,10},{9,11},{10,... | collective-permute-start | bytes 393224 | tf_op jit(solution)/shard_map/ppermute | solution.py:411
  16.7 11.5 %copy-start.5 = (bf16[128,2048]{1,0:T(8,128)(2,1)}, bf16[128,2048]{1,0:T(8,128)(2,1)S(1)}, u32[]{:S(2)}) copy-start(bf16[128,2048]{1,0:T(8,128)(2,1)S(1)} %collective-permute-done.3.refs_4_.refs_2_) | copy-start | bytes 1572868
  16.7 13.6 %collective-permute-start.12 = (bf16[128,2048]{1,0:T(8,128)(2,1)S(1)}, bf16[128,2048]{1,0:T(8,128)(2,1)}, u32[]{:S(2)}, u32[]{:S(2)}) collective-permute-start(bf16[128,2048]{1,0:T(8,128)(2,1)S(1)} %collective-permute-done.3.refs_4_.refs_2_), channel_id=1, source_target_pairs={{0,112},{8,120},{16,0},{24,8},{32,16},{40,24},{48,32},{56,40},{64,... | collective-permute-start | bytes 1572872 | tf_op jit(solution)/shard_map/ppermute | solution.py:408
  20.1 6.6 %collective-permute-start.17 = (f32[256,128]{1,0:T(8,128)S(1)}, f32[256,128]{1,0:T(8,128)S(1)}, u32[]{:S(2)}, u32[]{:S(2)}) collective-permute-start(f32[256,128]{1,0:T(8,128)S(1)} %add_add_fusion.1.part), channel_id=1, source_target_pairs={{0,1},{1,0},{2,3},{3,2},{4,5},{5,4},{6,7},{7,6},{8,9},{9,8},{10,11... | collective-permute-start | bytes 393224 | tf_op jit(solution)/shard_map/ppermute | solution.py:411
  28.2 7.4 %collective-permute-start.18 = (f32[1024,128]{1,0:T(8,128)S(1)}, f32[1024,128]{1,0:T(8,128)S(1)}, u32[]{:S(2)}, u32[]{:S(2)}) collective-permute-start(f32[1024,128]{1,0:T(8,128)S(1)} %get-tuple-element.26), channel_id=1, source_target_pairs={{0,8},{8,0},{16,24},{24,16},{32,40},{40,32},{48,56},{56,48},{64,72... | collective-permute-start | bytes 1572872 | tf_op jit(solution)/shard_map/ppermute | solution.py:408
  30.3 15.0 %collective-permute-start.19 = (bf16[128,2048]{1,0:T(8,128)(2,1)}, bf16[128,2048]{1,0:T(8,128)(2,1)S(1)}, u32[]{:S(2)}, u32[]{:S(2)}) collective-permute-start(bf16[128,2048]{1,0:T(8,128)(2,1)} %collective-permute-done.12.refs_4_), channel_id=1, source_target_pairs={{0,128},{8,136},{16,144},{24,152},{32,160},{40,168},{48,176},{56,1... | collective-permute-start | bytes 1572872 | tf_op jit(solution)/shard_map/ppermute | solution.py:408
  31.8 25.4 %collective-permute-start.10 = (bf16[256,2048]{1,0:T(8,128)(2,1)}, bf16[256,2048]{1,0:T(8,128)(2,1)S(1)}, u32[]{:S(2)}, u32[]{:S(2)}) collective-permute-start(bf16[256,2048]{1,0:T(8,128)(2,1)} %collective-permute-done.refs_0_.refs_2_), channel_id=1, source_target_pairs={{0,16},{8,24},{16,32},{24,40},{32,48},{40,56},{48,64},{56,72},{64,... | collective-permute-start | bytes 3145736 | tf_op jit(solution)/shard_map/ppermute | solution.py:408
  34.6 22.2 %collective-permute-start.4 = (bf16[128,2048]{1,0:T(8,128)(2,1)}, bf16[128,2048]{1,0:T(8,128)(2,1)}, u32[]{:S(2)}, u32[]{:S(2)}) collective-permute-start(bf16[128,2048]{1,0:T(8,128)(2,1)} %get-tuple-element.40), channel_id=1, source_target_pairs={{0,112},{8,120},{16,0},{24,8},{32,16},{40,24},{48,32},{56,40},{64,... | collective-permute-start | bytes 1572872 | tf_op jit(solution)/shard_map/ppermute | solution.py:408
  35.5 47.8 %collective-permute-start.2 = (bf16[256,2048]{1,0:T(8,128)(2,1)S(1)}, bf16[256,2048]{1,0:T(8,128)(2,1)}, u32[]{:S(2)}, u32[]{:S(2)}) collective-permute-start(bf16[256,2048]{1,0:T(8,128)(2,1)S(1)} %copy-done.1), channel_id=1, source_target_pairs={{0,8},{8,0},{16,24},{24,16},{32,40},{40,32},{48,56},{56,48},{64,72... | collective-permute-start | bytes 3145736 | tf_op jit(solution)/shard_map/ppermute | solution.py:408
  35.5 47.8 %collective-permute-start.5 = (bf16[256,2048]{1,0:T(8,128)(2,1)S(1)}, bf16[256,2048]{1,0:T(8,128)(2,1)}, u32[]{:S(2)}, u32[]{:S(2)}) collective-permute-start(bf16[256,2048]{1,0:T(8,128)(2,1)S(1)} %copy-done.1), channel_id=1, source_target_pairs={{0,128},{8,136},{16,144},{24,152},{32,160},{40,168},{48,176},{56,1... | collective-permute-start | bytes 3145736 | tf_op jit(solution)/shard_map/ppermute | solution.py:408
  45.3 0.8 copy-start.8
  46.1 37.2 %collective-permute-start.1 = (bf16[256,2048]{1,0:T(8,128)(2,1)}, bf16[256,2048]{1,0:T(8,128)(2,1)}, u32[]{:S(2)}, u32[]{:S(2)}) collective-permute-start(bf16[256,2048]{1,0:T(8,128)(2,1)} %collective-permute-done.refs_0_.refs_2_), channel_id=1, source_target_pairs={{0,8},{8,0},{16,24},{24,16},{32,40},{40,32},{48,56},{56,48},{64,72... | collective-permute-start | bytes 3145736 | tf_op jit(solution)/shard_map/ppermute | solution.py:408
  47.0 48.6 %all-to-all-start = ((f32[16,64,128]{2,1,0:T(8,128)}), f32[16,64,128]{2,1,0:T(8,128)S(1)}, u32[]{:S(2)}, u32[]{:S(2)}) async-start(f32[16,64,128]{2,1,0:T(8,128)} %bitcast.20), calls=%async_computation | async-start | bytes 1048576 | tf_op jit(solution)/shard_map/all_to_all | solution.py:215
  56.7 25.1 %collective-permute-start.13 = (bf16[128,2048]{1,0:T(8,128)(2,1)}, bf16[128,2048]{1,0:T(8,128)(2,1)}, u32[]{:S(2)}, u32[]{:S(2)}) collective-permute-start(bf16[128,2048]{1,0:T(8,128)(2,1)} %collective-permute-done.4.refs_5_.refs_3_), channel_id=1, source_target_pairs={{0,112},{8,120},{16,0},{24,8},{32,16},{40,24},{48,32},{56,40},{64,... | collective-permute-start | bytes 1572872 | tf_op jit(solution)/shard_map/ppermute | solution.py:408
  57.2 46.1 %collective-permute-start.11 = (bf16[256,2048]{1,0:T(8,128)(2,1)S(1)}, bf16[256,2048]{1,0:T(8,128)(2,1)}, u32[]{:S(2)}, u32[]{:S(2)}) collective-permute-start(bf16[256,2048]{1,0:T(8,128)(2,1)S(1)} %collective-permute-done.10.refs_0_), channel_id=1, source_target_pairs={{0,8},{8,0},{16,24},{24,16},{32,40},{40,32},{48,56},{56,48},{64,72... | collective-permute-start | bytes 3145736 | tf_op jit(solution)/shard_map/ppermute | solution.py:408
  81.8 25.6 %collective-permute-start.20 = (bf16[128,2048]{1,0:T(8,128)(2,1)}, bf16[128,2048]{1,0:T(8,128)(2,1)}, u32[]{:S(2)}, u32[]{:S(2)}) collective-permute-start(bf16[128,2048]{1,0:T(8,128)(2,1)} %collective-permute-done.13.refs_5_), channel_id=1, source_target_pairs={{0,128},{8,136},{16,144},{24,152},{32,160},{40,168},{48,176},{56,1... | collective-permute-start | bytes 1572872 | tf_op jit(solution)/shard_map/ppermute | solution.py:408
  83.3 1.0 copy-start.6
  90.7 0.8 copy-start.3
  91.6 31.3 %collective-permute-start.8 = (f32[576,256]{1,0:T(8,128)}, f32[576,256]{1,0:T(8,128)}, u32[]{:S(2)}, u32[]{:S(2)}) collective-permute-start(f32[576,256]{1,0:T(8,128)} %get-tuple-element.24), channel_id=1, source_target_pairs={{0,6},{1,7},{2,4},{3,5},{4,2},{5,3},{6,0},{7,1},{8,14},{9,15},{10,... | collective-permute-start | bytes 1769480 | tf_op jit(solution)/shard_map/ppermute | solution.py:411
  94.6 28.9 %collective-permute-start.7 = (f32[576,256]{1,0:T(8,128)}, f32[576,256]{1,0:T(8,128)}, u32[]{:S(2)}, u32[]{:S(2)}) collective-permute-start(f32[576,256]{1,0:T(8,128)} %get-tuple-element.23), channel_id=1, source_target_pairs={{0,4},{1,5},{2,6},{3,7},{4,0},{5,1},{6,2},{7,3},{8,12},{9,13},{10,... | collective-permute-start | bytes 1769480 | tf_op jit(solution)/shard_map/ppermute | solution.py:411
  95.2 28.2 %collective-permute-start.6 = (f32[576,256]{1,0:T(8,128)}, f32[576,256]{1,0:T(8,128)}, u32[]{:S(2)}, u32[]{:S(2)}) collective-permute-start(f32[576,256]{1,0:T(8,128)} %get-tuple-element.22), channel_id=1, source_target_pairs={{0,2},{1,3},{2,0},{3,1},{4,6},{5,7},{6,4},{7,5},{8,10},{9,11},{10,... | collective-permute-start | bytes 1769480 | tf_op jit(solution)/shard_map/ppermute | solution.py:411
  96.3 0.8 copy-start.2
  97.1 38.5 %all-to-all-start.1 = ((f32[16,64,128]{2,1,0:T(8,128)}), f32[16,64,128]{2,1,0:T(8,128)S(1)}, u32[]{:S(2)}, u32[]{:S(2)}) async-start(f32[16,64,128]{2,1,0:T(8,128)} %copy-done.2), calls=%async_computation.1 | async-start | bytes 1048576 | tf_op jit(solution)/shard_map/all_to_all | solution.py:215
  103.3 1.0 copy-start.7
  104.4 3.1 %copy-start.9 = (bf16[128,2048]{1,0:T(8,128)(2,1)S(1)}, bf16[128,2048]{1,0:T(8,128)(2,1)}, u32[]{:S(2)}) copy-start(bf16[128,2048]{1,0:T(8,128)(2,1)} %copy-done.8) | copy-start | bytes 1572868
  107.4 16.0 %copy-start.4 = (f32[576,256]{1,0:T(8,128)S(1)}, f32[576,256]{1,0:T(8,128)}, u32[]{:S(2)}) copy-start(f32[576,256]{1,0:T(8,128)} %copy-done.3) | copy-start | bytes 1769476
  112.3 12.4 %copy-start.10 = (f32[4,96,256]{2,1,0:T(8,128)}, f32[4,96,256]{2,1,0:T(8,128)S(1)}, u32[]{:S(2)}) copy-start(f32[4,96,256]{2,1,0:T(8,128)S(1)} %get-tuple-element.32) | copy-start | bytes 1179652
  112.3 19.9 %collective-permute-start.22 = (f32[2,160,256]{2,1,0:T(8,128)S(1)}, f32[2,160,256]{2,1,0:T(8,128)S(1)}, u32[]{:S(2)}, u32[]{:S(2)}) collective-permute-start(f32[2,160,256]{2,1,0:T(8,128)S(1)} %get-tuple-element.30), channel_id=1, source_target_pairs={{0,4},{1,5},{2,6},{3,7},{4,0},{5,1},{6,2},{7,3},{8,12},{9,13},{10,... | collective-permute-start | bytes 983048 | tf_op jit(solution)/shard_map/ppermute | solution.py:411
  115.5 18.6 %collective-permute-start.23 = (f32[2,160,256]{2,1,0:T(8,128)S(1)}, f32[2,160,256]{2,1,0:T(8,128)S(1)}, u32[]{:S(2)}, u32[]{:S(2)}) collective-permute-start(f32[2,160,256]{2,1,0:T(8,128)S(1)} %get-tuple-element.31), channel_id=1, source_target_pairs={{0,6},{1,7},{2,4},{3,5},{4,2},{5,3},{6,0},{7,1},{8,14},{9,15},{10,... | collective-permute-start | bytes 983048 | tf_op jit(solution)/shard_map/ppermute | solution.py:411
  122.8 11.9 %collective-permute-start.21 = (f32[2,160,256]{2,1,0:T(8,128)S(1)}, f32[2,160,256]{2,1,0:T(8,128)S(1)}, u32[]{:S(2)}, u32[]{:S(2)}) collective-permute-start(f32[2,160,256]{2,1,0:T(8,128)S(1)} %get-tuple-element.29), channel_id=1, source_target_pairs={{0,2},{1,3},{2,0},{3,1},{4,6},{5,7},{6,4},{7,5},{8,10},{9,11},{10,... | collective-permute-start | bytes 983048 | tf_op jit(solution)/shard_map/ppermute | solution.py:411
  124.7 24.6 %collective-permute-start.9 = (f32[320,256]{1,0:T(8,128)S(1)}, f32[320,256]{1,0:T(8,128)S(1)}, u32[]{:S(2)}, u32[]{:S(2)}) collective-permute-start(f32[320,256]{1,0:T(8,128)S(1)} %fusion.one), channel_id=1, source_target_pairs={{0,1},{1,0},{2,3},{3,2},{4,5},{5,4},{6,7},{7,6},{8,9},{9,8},{10,11... | collective-permute-start | bytes 983048 | tf_op jit(solution)/shard_map/ppermute | solution.py:411
  127.5 13.4 %collective-permute-start.25 = (f32[4,96,256]{2,1,0:T(8,128)}, f32[4,96,256]{2,1,0:T(8,128)}, u32[]{:S(2)}, u32[]{:S(2)}) collective-permute-start(f32[4,96,256]{2,1,0:T(8,128)} %get-tuple-element.33), channel_id=1, source_target_pairs={{0,1},{1,0},{2,3},{3,2},{4,5},{5,4},{6,7},{7,6},{8,9},{9,8},{10,11... | collective-permute-start | bytes 1179656 | tf_op jit(solution)/shard_map/ppermute | solution.py:411
  135.5 5.4 %copy-start.11 = (f32[4,96,256]{2,1,0:T(8,128)S(1)}, f32[4,96,256]{2,1,0:T(8,128)}, u32[]{:S(2)}) copy-start(f32[4,96,256]{2,1,0:T(8,128)} %copy-done.10) | copy-start | bytes 1179652
  135.5 14.3 %collective-permute-start.33 = (f32[1024,128]{1,0:T(8,128)S(1)}, f32[1024,128]{1,0:T(8,128)S(1)}, u32[]{:S(2)}, u32[]{:S(2)}) collective-permute-start(f32[1024,128]{1,0:T(8,128)S(1)} %bitcast.18), channel_id=1, source_target_pairs={{0,8},{8,0},{16,24},{24,16},{32,40},{40,32},{48,56},{56,48},{64,72... | collective-permute-start | bytes 1572872 | tf_op jit(solution)/shard_map/ppermute | solution.py:408
  136.6 15.5 %collective-permute-start.24 = (f32[160,256]{1,0:T(8,128)S(1)}, f32[160,256]{1,0:T(8,128)S(1)}, u32[]{:S(2)}, u32[]{:S(2)}) collective-permute-start(f32[160,256]{1,0:T(8,128)S(1)} %get-tuple-element.46), channel_id=1, source_target_pairs={{0,1},{1,0},{2,3},{3,2},{4,5},{5,4},{6,7},{7,6},{8,9},{9,8},{10,11... | collective-permute-start | bytes 491528 | tf_op jit(solution)/shard_map/ppermute | solution.py:411
  142.0 13.5 %collective-permute-start.26 = (f32[96,256]{1,0:T(8,128)S(1)}, f32[96,256]{1,0:T(8,128)S(1)}, u32[]{:S(2)}, u32[]{:S(2)}) collective-permute-start(f32[96,256]{1,0:T(8,128)S(1)} %get-tuple-element.44), channel_id=1, source_target_pairs={{0,2},{1,3},{2,0},{3,1},{4,6},{5,7},{6,4},{7,5},{8,10},{9,11},{10,... | collective-permute-start | bytes 294920 | tf_op jit(solution)/shard_map/ppermute | solution.py:411
  143.9 13.4 %collective-permute-start.27 = (f32[96,256]{1,0:T(8,128)S(1)}, f32[96,256]{1,0:T(8,128)S(1)}, u32[]{:S(2)}, u32[]{:S(2)}) collective-permute-start(f32[96,256]{1,0:T(8,128)S(1)} %get-tuple-element.43), channel_id=1, source_target_pairs={{0,4},{1,5},{2,6},{3,7},{4,0},{5,1},{6,2},{7,3},{8,12},{9,13},{10,... | collective-permute-start | bytes 294920 | tf_op jit(solution)/shard_map/ppermute | solution.py:411
  149.4 9.2 %collective-permute-start.28 = (f32[96,256]{1,0:T(8,128)S(1)}, f32[96,256]{1,0:T(8,128)S(1)}, u32[]{:S(2)}, u32[]{:S(2)}) collective-permute-start(f32[96,256]{1,0:T(8,128)S(1)} %get-tuple-element.42), channel_id=1, source_target_pairs={{0,6},{1,7},{2,4},{3,5},{4,2},{5,3},{6,0},{7,1},{8,14},{9,15},{10,... | collective-permute-start | bytes 294920 | tf_op jit(solution)/shard_map/ppermute | solution.py:411
  151.2 18.9 %collective-permute-start.34 = (f32[384,128]{1,0:T(8,128)S(1)}, f32[384,128]{1,0:T(8,128)S(1)}, u32[]{:S(2)}, u32[]{:S(2)}) collective-permute-start(f32[384,128]{1,0:T(8,128)S(1)} %shard_map.56.refs_4_), channel_id=1, source_target_pairs={{0,2},{1,3},{2,0},{3,1},{4,6},{5,7},{6,4},{7,5},{8,10},{9,11},{10,... | collective-permute-start | bytes 589832 | tf_op jit(solution)/shard_map/ppermute | solution.py:411
  152.1 19.9 %collective-permute-start.35 = (f32[384,128]{1,0:T(8,128)S(1)}, f32[384,128]{1,0:T(8,128)S(1)}, u32[]{:S(2)}, u32[]{:S(2)}) collective-permute-start(f32[384,128]{1,0:T(8,128)S(1)} %shard_map.56.refs_4_), channel_id=1, source_target_pairs={{0,4},{1,5},{2,6},{3,7},{4,0},{5,1},{6,2},{7,3},{8,12},{9,13},{10,... | collective-permute-start | bytes 589832 | tf_op jit(solution)/shard_map/ppermute | solution.py:411
  155.5 19.8 %collective-permute-start.36 = (f32[384,128]{1,0:T(8,128)S(1)}, f32[384,128]{1,0:T(8,128)S(1)}, u32[]{:S(2)}, u32[]{:S(2)}) collective-permute-start(f32[384,128]{1,0:T(8,128)S(1)} %shard_map.56.refs_4_), channel_id=1, source_target_pairs={{0,6},{1,7},{2,4},{3,5},{4,2},{5,3},{6,0},{7,1},{8,14},{9,15},{10,... | collective-permute-start | bytes 589832 | tf_op jit(solution)/shard_map/ppermute | solution.py:411
  159.3 16.5 %collective-permute-start.29 = (bf16[256,256]{1,0:T(8,128)(2,1)S(1)}, bf16[256,256]{1,0:T(8,128)(2,1)S(1)}, u32[]{:S(2)}, u32[]{:S(2)}) collective-permute-start(bf16[256,256]{1,0:T(8,128)(2,1)S(1)} %get-tuple-element.34), channel_id=1, source_target_pairs={{139,228},{168,76},{201,109},{234,14},{7,35},{5,163},{8,27},{23,12... | collective-permute-start | bytes 393224 | tf_op jit(solution)/shard_map/ppermute | solution.py:507
  161.2 14.5 %collective-permute-start.30 = (bf16[256,256]{1,0:T(8,128)(2,1)S(1)}, bf16[256,256]{1,0:T(8,128)(2,1)S(1)}, u32[]{:S(2)}, u32[]{:S(2)}) collective-permute-start(bf16[256,256]{1,0:T(8,128)(2,1)S(1)} %get-tuple-element.35), channel_id=1, source_target_pairs={{3,124},{1,96},{4,163},{13,171},{18,1},{16,35},{23,176},{21,179},{... | collective-permute-start | bytes 393224 | tf_op jit(solution)/shard_map/ppermute | solution.py:507
  170.1 10.5 %collective-permute-start.31 = (bf16[256,256]{1,0:T(8,128)(2,1)S(1)}, bf16[256,256]{1,0:T(8,128)(2,1)S(1)}, u32[]{:S(2)}, u32[]{:S(2)}) collective-permute-start(bf16[256,256]{1,0:T(8,128)(2,1)S(1)} %get-tuple-element.36), channel_id=1, source_target_pairs={{37,192},{44,200},{77,233},{144,52},{193,170},{7,120},{0,19},{31,1... | collective-permute-start | bytes 393224 | tf_op jit(solution)/shard_map/ppermute | solution.py:507
  172.1 8.6 %collective-permute-start.32 = (bf16[256,256]{1,0:T(8,128)(2,1)S(1)}, bf16[256,256]{1,0:T(8,128)(2,1)S(1)}, u32[]{:S(2)}, u32[]{:S(2)}) collective-permute-start(bf16[256,256]{1,0:T(8,128)(2,1)S(1)} %get-tuple-element.37), channel_id=1, source_target_pairs={{15,171},{20,176},{103,130},{110,138},{24,43},{34,17},{32,1},{38,1... | collective-permute-start | bytes 393224 | tf_op jit(solution)/shard_map/ppermute | solution.py:507
  175.4 7.0 %collective-permute-start.37 = (f32[256,128]{1,0:T(8,128)S(1)}, f32[256,128]{1,0:T(8,128)S(1)}, u32[]{:S(2)}, u32[]{:S(2)}) collective-permute-start(f32[256,128]{1,0:T(8,128)S(1)} %fusion.2.refs_8_), channel_id=1, source_target_pairs={{0,1},{1,0},{2,3},{3,2},{4,5},{5,4},{6,7},{7,6},{8,9},{9,8},{10,11... | collective-permute-start | bytes 393224 | tf_op jit(solution)/shard_map/ppermute | solution.py:411
